TPU v7x, 32 devices: a whole 2x2x4 slice. The times are simulated.
32 devices in a mesh: groups: 2 (over x), req: 8 (over z, y), head: 2 (over core).
Axes of the slice: x: 2, y: 2, z: 4, core: 2. Of those that a mesh axis runs over, the one named last changes fastest.
Arguments:
- queries: bfloat16 [2048, 32, 128], P(('groups', 'req'), 'head'), parts along dimension 0, may hold values from -100 to 100
- new_keys: bfloat16 [2048, 2, 128], P(('groups', 'req'), 'head'), parts along dimension 0, may hold values from -4.5 to 4.5
- new_values: bfloat16 [2048, 2, 128], P(('groups', 'req'), 'head'), parts along dimension 0, may hold values from -6 to 6
- cluster_kv: bfloat16 [1024, 2, 2, 128, 128], P(('groups', 'req'), 'head'), parts along dimension 0, may hold values from -6 to 6
- cluster_len: int32 [32], P('groups'), parts along dimension 0, may hold values from 1 to 4096, 40960 in all
- piece_slot: int32 [32, 32], P('groups'), parts along dimension 0, may hold values from 0 to 511, as said below
- cluster_ids: int32 [16, 2, 2], P('groups', 'head'), parts along dimension 0, may hold values from 0 to 15, all different within a row
- w_out: bfloat16 [4096, 4096], P('head', 'req'), may hold values from -0.09375 to 0.09375
Outputs:
- projected: bfloat16 [2048, 4096], P(('groups', 'req', 'head')), parts along dimension 0
There are 2 independent parts, one for each index of `groups`. A program takes and returns all parts, laid end to end along the dimension named above; an argument that names none is the same for every part. Nothing has to cross between parts.
Inputs may be any that keep to these rules, and one draw needn't show every extreme that they name: `cluster_ids`: for each request and KV head, 2 distinct cluster numbers. A permutation of the slots: piece p of cluster c lies in slot piece_slot[c, p], stored on index slot // 64 of req, and every cluster has exactly 4 of its pieces on every index of req.
All inputs are finite; a program needn't handle non-finite values.
Results may differ from a plain program's by a relative error of at most 0.0052.
Values may be sent and summed in bfloat16 or wider, within the bound.
A program may use at most 128 MiB of HBM per device.

v0:
```python
import functools

import jax
import jax.numpy as jnp
from jax import lax
from jax.experimental import pallas as pl
from jax.experimental.pallas import tpu as pltpu
from jax.sharding import PartitionSpec as P

MESH = pl.DeviceIdType.MESH
NEG = -1e30
LOG2E = 1.4426950408889634


def pick_kernel(peers, ids_ref, slot_ref, len_ref, kv_ref, send_ref, lim_ref, pick, count, held_pieces, in_sem, out_sem):
    me = lax.axis_index("req")
    held, _, _, piece_keys, _ = kv_ref.shape
    sel = ids_ref.shape[2]
    pieces = slot_ref.shape[1]
    per = pieces // peers
    base = me * held

    @pl.loop(0, peers)
    def _(r):
        for s in range(sel):
            c = ids_ref[r, 0, s]
            n = jnp.int32(0)
            for p in range(pieces):
                loc = slot_ref[c, p] - base
                pick[n] = loc
                n = n + ((loc >= 0) & (loc < held)).astype(jnp.int32)
            for j in range(per):
                pltpu.make_async_copy(kv_ref.at[pick[j], 0], held_pieces.at[r, s * per + j], in_sem.at[r]).start()

    for s in range(sel):
        c = ids_ref[me, 0, s]
        fill = len_ref[c]
        for o in range(peers):
            count[o] = 0
        for p in range(pieces):
            o = slot_ref[c, p] // held
            j = count[o]
            lim_ref[o, s * per + j] = fill - p * piece_keys
            count[o] = j + 1

    def put(r):
        return pltpu.make_async_copy(held_pieces.at[r], send_ref.at[r], out_sem.at[r])

    @pl.loop(0, peers)
    def _(r):
        pltpu.make_async_copy(send_ref.at[r], held_pieces.at[r], in_sem.at[r]).wait()
        put(r).start()

    @pl.loop(0, peers)
    def _(r):
        put(r).wait()


def attend_kernel(peers, heads, lim_ref, send_ref, q_ref, k_ref, v_ref, w_ref, out_ref, w_pair_ref,
                  recv, qt, top, total, acc, send_sem, recv_sem, w_sem, own_sem):
    me = lax.axis_index("req")
    tok = q_ref.shape[0]
    hd = k_ref.shape[1]
    count = send_ref.shape[1]
    piece_keys = send_ref.shape[3]
    rows = heads * tok
    block = min(128, rows)
    phases = send_sem.shape[1]
    group = count // phases
    factor = hd ** (-0.5) * LOG2E

    own_copy = pltpu.make_async_copy(send_ref.at[me], recv.at[me], own_sem)
    own_copy.start()
    barrier = pltpu.get_barrier_semaphore()
    for k in range(1, peers):
        pl.semaphore_signal(barrier, inc=1, device_id={"req": lax.rem(me + k, peers)}, device_id_type=MESH)
    pl.semaphore_wait(barrier, peers - 1)

    def peer_of(i):
        off = jnp.where(i % 2 == 1, (i + 1) // 2, peers - i // 2)
        return lax.rem(me + off, peers)

    def copy_to(peer, f):
        part = pl.ds(f * group, group)
        return pltpu.make_async_remote_copy(
            src_ref=send_ref.at[peer, part], dst_ref=recv.at[me, part],
            send_sem=send_sem.at[peer, f], recv_sem=recv_sem.at[me, f],
            device_id={"req": peer}, device_id_type=MESH)

    def copy_from(peer, f):
        part = pl.ds(f * group, group)
        return pltpu.make_async_remote_copy(
            src_ref=send_ref.at[peer, part], dst_ref=recv.at[peer, part],
            send_sem=send_sem.at[peer, f], recv_sem=recv_sem.at[peer, f],
            device_id={"req": peer}, device_id_type=MESH)

    @pl.loop(0, phases)
    def _(f):
        @pl.loop(1, peers)
        def _(i):
            copy_to(peer_of(i), f).start()

    pair_copy = pltpu.make_async_remote_copy(
        src_ref=w_ref, dst_ref=w_pair_ref, send_sem=w_sem.at[0], recv_sem=w_sem.at[1],
        device_id={"req": me + 1 - 2 * (me % 2)}, device_id_type=MESH)
    pair_copy.start()

    for h in range(heads):
        qt[:, h * tok:(h + 1) * tok] = q_ref[:, h, :].T
    own_vt = v_ref[...].T

    @pl.loop(0, rows // block)
    def _(b):
        cols = pl.ds(pl.multiple_of(b * block, block), block)
        s = jnp.dot(k_ref[...], qt[:, cols], preferred_element_type=jnp.float32)
        u = lax.broadcasted_iota(jnp.int32, s.shape, 0)
        t = lax.broadcasted_iota(jnp.int32, s.shape, 1) % tok
        s = jnp.where(u <= t, s, NEG)
        m = jnp.max(s, axis=0, keepdims=True)
        w = jnp.exp2((s - m) * factor)
        top[:, cols] = m
        total[:, cols] = jnp.sum(w, axis=0, keepdims=True)
        acc[:, cols] = jnp.dot(own_vt, w.astype(jnp.bfloat16), preferred_element_type=jnp.float32)

    def attend(src_ref, peer, f):
        keys = group * piece_keys
        k = src_ref[peer, pl.ds(f * group, group), 0].reshape(keys, hd)
        vt = jnp.concatenate([src_ref[peer, f * group + i, 1].T for i in range(group)], axis=1)
        fills = [lim_ref[peer, f * group + i] for i in range(group)]
        key = lax.broadcasted_iota(jnp.int32, (piece_keys, block), 0)

        def score(b):
            s = jnp.dot(k, qt[:, b * block:(b + 1) * block], preferred_element_type=jnp.float32)
            return jnp.concatenate(
                [jnp.where(key < fills[i], s[i * piece_keys:(i + 1) * piece_keys], NEG) for i in range(group)], axis=0)

        def weigh(b, s):
            cols = slice(b * block, (b + 1) * block)
            m_old = top[:, cols]
            m = jnp.maximum(m_old, jnp.max(s, axis=0, keepdims=True))
            keep = jnp.exp2((m_old - m) * factor)
            w = jnp.exp2((s - m) * factor)
            mixed = jnp.dot(vt, w.astype(jnp.bfloat16), preferred_element_type=jnp.float32)
            top[:, cols] = m
            total[:, cols] = total[:, cols] * keep + jnp.sum(w, axis=0, keepdims=True)
            acc[:, cols] = acc[:, cols] * keep + mixed

        s = score(0)
        for b in range(rows // block):
            ahead = score(b + 1) if b + 1 < rows // block else None
            weigh(b, s)
            s = ahead

    own_copy.wait()

    @pl.loop(0, phases)
    def _(f):
        attend(recv, me, f)

    @pl.loop(0, phases * (peers - 1))
    def _(step):
        f = step // (peers - 1)
        peer = peer_of(step % (peers - 1) + 1)
        copy_from(peer, f).wait_recv()
        attend(recv, peer, f)

    for h in range(heads):
        rows_h = slice(h * tok, (h + 1) * tok)
        o = acc[:, rows_h] / total[:, rows_h]
        out_ref[:, h * hd:(h + 1) * hd] = o.T.astype(out_ref.dtype)

    @pl.loop(0, phases)
    def _(f):
        @pl.loop(1, peers)
        def _(i):
            copy_to(peer_of(i), f).wait_send()

    pair_copy.wait()


def project_kernel(far, att_ref, w_ref, w_pair_ref, out_ref,
                   full, wv, part, got, low, load_sem, send_sem, recv_sem,
                   part_send, part_recv, out_send, out_recv):
    me = lax.axis_index("req")
    head = lax.axis_index("head")
    hi, lo = me // 2, me % 2
    half = out_ref.shape[0]
    columns = w_ref.shape[1]
    wide = 2 * columns

    def at(z):
        return {"req": z * 2 + lo}

    load_own = pltpu.make_async_copy(att_ref, full.at[hi], load_sem.at[0])
    load_w = pltpu.make_async_copy(w_ref, wv.at[lo], load_sem.at[1])
    load_pair = pltpu.make_async_copy(w_pair_ref, wv.at[1 - lo], load_sem.at[2])
    load_own.start()
    load_w.start()
    load_pair.start()

    barrier = pltpu.get_barrier_semaphore()
    for k in range(1, far):
        pl.semaphore_signal(barrier, inc=1, device_id=at(lax.rem(hi + k, far)), device_id_type=MESH)
    pl.semaphore_signal(barrier, inc=1, device_id={"head": 1 - head}, device_id_type=MESH)
    pl.semaphore_wait(barrier, far)

    def block_copy(z, to, way):
        return pltpu.make_async_remote_copy(
            src_ref=full.at[z], dst_ref=full.at[z], send_sem=send_sem.at[way, z],
            recv_sem=recv_sem.at[z], device_id=at(to), device_id_type=MESH)

    def part_copy(z):
        return pltpu.make_async_remote_copy(
            src_ref=part.at[z, 1 - head], dst_ref=got.at[z], send_sem=part_send.at[z],
            recv_sem=part_recv.at[z], device_id={"head": 1 - head}, device_id_type=MESH)

    def out_copy(z, owner):
        return pltpu.make_async_remote_copy(
            src_ref=low.at[z], dst_ref=out_ref.at[:, pl.ds(pl.multiple_of(owner * wide, wide), wide)],
            send_sem=out_send.at[z], recv_sem=out_recv.at[owner], device_id=at(z), device_id_type=MESH)

    def compute(z):
        @pl.loop(0, 2)
        def _(j):
            cols = pl.ds(pl.multiple_of(j * columns, columns), columns)
            terms = jnp.dot(full[z], wv[j], preferred_element_type=jnp.float32)
            part[z, 0, :, cols] = terms[:half]
            part[z, 1, :, cols] = terms[half:]
        part_copy(z).start()

    def finish(z):
        part_copy(z).wait_recv()
        rows = (part[z, head] + got[z]).astype(out_ref.dtype)

        @pl.when(z == hi)
        def _():
            out_ref[:, pl.ds(pl.multiple_of(hi * wide, wide), wide)] = rows

        @pl.when(z != hi)
        def _():
            low[z] = rows
            out_copy(z, hi).start()

    load_own.wait()

    @pl.when(hi < far - 1)
    def _():
        block_copy(hi, hi + 1, 0).start()

    @pl.when(hi > 0)
    def _():
        block_copy(hi, hi - 1, 1).start()

    load_w.wait()
    load_pair.wait()
    compute(hi)

    @pl.loop(1, far + 1)
    def _(d):
        @pl.when((hi - d >= 0) & (d < far))
        def _():
            block_copy(hi - d, hi, 0).wait_recv()

            @pl.when(hi < far - 1)
            def _():
                block_copy(hi - d, hi + 1, 0).start()

        @pl.when(hi + d < far)
        def _():
            block_copy(hi + d, hi, 1).wait_recv()

            @pl.when(hi > 0)
            def _():
                block_copy(hi + d, hi - 1, 1).start()

        @pl.loop(0, 2)
        def _(side):
            z = hi + d * (2 * side - 1)

            @pl.when((z >= 0) & (z < far))
            def _():
                compute(z)

        @pl.loop(0, 2)
        def _(side):
            z = hi + (d - 1) * (2 * side - 1)

            @pl.when((z >= 0) & (z < far) & ((d > 1) | (side == 0)))
            def _():
                finish(z)

    @pl.loop(0, far)
    def _(z):
        @pl.when((z <= hi) & (hi < far - 1))
        def _():
            block_copy(z, hi + 1, 0).wait_send()

        @pl.when((z >= hi) & (hi > 0))
        def _():
            block_copy(z, hi - 1, 1).wait_send()

        part_copy(z).wait_send()

        @pl.when(z != hi)
        def _():
            out_copy(z, hi).wait_send()
            out_copy(z, z).wait_recv()


def local(queries, new_keys, new_values, cluster_kv, cluster_len, piece_slot, cluster_ids, w_out):
    peers = lax.axis_size("req")
    tok, heads, hd = queries.shape
    piece_keys = cluster_kv.shape[3]
    pieces = piece_slot.shape[1]
    sel = cluster_ids.shape[2]
    count = sel * (pieces // peers)
    vmem = pl.BlockSpec(memory_space=pltpu.VMEM)
    smem = pl.BlockSpec(memory_space=pltpu.SMEM)
    any_space = pl.BlockSpec(memory_space=pltpu.HBM)
    send, lim = pl.pallas_call(
        functools.partial(pick_kernel, peers),
        out_shape=(
            jax.ShapeDtypeStruct((peers, count, 2, piece_keys, hd), cluster_kv.dtype),
            jax.ShapeDtypeStruct((peers, count), jnp.int32),
        ),
        in_specs=[smem, smem, smem, any_space],
        out_specs=(any_space, smem),
        scratch_shapes=[
            pltpu.SMEM((pieces + 1,), jnp.int32),
            pltpu.SMEM((peers,), jnp.int32),
            pltpu.VMEM((peers, count, 2, piece_keys, hd), cluster_kv.dtype),
            pltpu.SemaphoreType.DMA((peers,)),
            pltpu.SemaphoreType.DMA((peers,)),
        ],
        name="pick",
    )(cluster_ids, piece_slot, cluster_len, cluster_kv)
    rows = heads * tok
    phases = min(4, count)
    attended, w_pair = pl.pallas_call(
        functools.partial(attend_kernel, peers, heads),
        out_shape=(
            jax.ShapeDtypeStruct((tok, heads * hd), jnp.bfloat16),
            jax.ShapeDtypeStruct(w_out.shape, w_out.dtype),
        ),
        in_specs=[smem, any_space, vmem, vmem, vmem, any_space],
        out_specs=(vmem, any_space),
        scratch_shapes=[
            pltpu.VMEM((peers, count, 2, piece_keys, hd), cluster_kv.dtype),
            pltpu.VMEM((hd, rows), jnp.bfloat16),
            pltpu.VMEM((1, rows), jnp.float32),
            pltpu.VMEM((1, rows), jnp.float32),
            pltpu.VMEM((hd, rows), jnp.float32),
            pltpu.SemaphoreType.DMA((peers, phases)),
            pltpu.SemaphoreType.DMA((peers, phases)),
            pltpu.SemaphoreType.DMA((2,)),
            pltpu.SemaphoreType.DMA,
        ],
        compiler_params=pltpu.CompilerParams(
            collective_id=0, has_side_effects=True, vmem_limit_bytes=60 * 2**20),
        name="attend",
    )(lim, send, queries, new_keys[:, 0], new_values[:, 0], w_out)
    far = peers // 2
    half = tok // lax.axis_size("head")
    depth, columns = w_out.shape
    return pl.pallas_call(
        functools.partial(project_kernel, far),
        out_shape=jax.ShapeDtypeStruct((half, peers * columns), jnp.bfloat16),
        in_specs=[any_space, any_space, any_space],
        out_specs=vmem,
        scratch_shapes=[
            pltpu.VMEM((far, tok, depth), jnp.bfloat16),
            pltpu.VMEM((2, depth, columns), w_out.dtype),
            pltpu.VMEM((far, 2, half, 2 * columns), jnp.float32),
            pltpu.VMEM((far, half, 2 * columns), jnp.float32),
            pltpu.VMEM((far, half, 2 * columns), jnp.bfloat16),
            pltpu.SemaphoreType.DMA((3,)),
            pltpu.SemaphoreType.DMA((2, far)),
            pltpu.SemaphoreType.DMA((far,)),
            pltpu.SemaphoreType.DMA((far,)),
            pltpu.SemaphoreType.DMA((far,)),
            pltpu.SemaphoreType.DMA((far,)),
            pltpu.SemaphoreType.DMA((far,)),
        ],
        compiler_params=pltpu.CompilerParams(
            collective_id=1, has_side_effects=True, vmem_limit_bytes=60 * 2**20),
        name="project",
    )(attended, w_out, w_pair)


def solution(mesh):
    return jax.shard_map(
        local,
        mesh=mesh,
        in_specs=(
            P(("groups", "req"), "head", None),
            P(("groups", "req"), "head", None),
            P(("groups", "req"), "head", None),
            P(("groups", "req"), "head", None, None, None),
            P("groups"),
            P("groups", None),
            P("groups", "head", None),
            P("head", "req"),
        ),
        out_specs=P(("groups", "req", "head"), None),
        check_vma=False,
    )
```

profile of v0, /device:TPU:0, one launch (start us, length us, event | category | flops | bytes accessed | tf_op | source)
XLA Modules:
  0.0 160.9 jit_solution(17511023393083701561)
XLA Ops:
  0.0 1.3 copy.9.ids_ref
  1.3 5.7 %pick.1 = (bf16[8,8,2,128,128]{4,3,2,1,0:T(8,128)(2,1)}, s32[8,8]{1,0:T(8,128)}) custom-call(s32[8,1,2]{2,1,0:T(1,128)} %copy.9.ids_ref, s32[16,32]{1,0:T(8,128)} %slot_ref.1, s32[16]{0:T(128)} %len_ref.1, bf16[64,1,2,128,128]{4,3,2,1,0:T(8,128)(2,1)} %kv_ref.1), custom_call_target="tpu_custom_call" | custom-call | tf_op jit(solution)/shard_map/pick/pallas_call | solution.py:320
  7.1 101.6 %attend.1 = (bf16[128,2048]{1,0:T(8,128)(2,1)}, bf16[2048,512]{1,0:T(8,128)(2,1)}) custom-call(s32[8,8]{1,0:T(8,128)} %get-tuple-element.9.lim_ref, bf16[8,8,2,128,128]{4,3,2,1,0:T(8,128)(2,1)} %get-tuple-element.10.send_ref, bf16[128,16,128]{2,1,0:T(8,128)(2,1)} %q_ref.1, bf16[128,128]{1,0:T(8,128)(2,1)} %bitcast.2, bf16[128,128]{1,0:T(8,128)(2,1)} %bitcast.3, ...), custom_call_target="tpu_custom_call" | custom-call | tf_op jit(solution)/shard_map/attend/pallas_call | solution.py:339
  108.7 50.4 %project.1 = bf16[64,4096]{1,0:T(8,128)(2,1)} custom-call(bf16[128,2048]{1,0:T(8,128)(2,1)} %get-tuple-element.11.att_ref, bf16[2048,512]{1,0:T(8,128)(2,1)} %w_ref.3, bf16[2048,512]{1,0:T(8,128)(2,1)} %get-tuple-element.12.w_pair_ref), custom_call_target="tpu_custom_call" | custom-call | tf_op jit(solution)/shard_map/project/pallas_call | solution.py:365
  159.0 1.9 %copy.11 = bf16[64,4096]{1,0:T(8,128)(2,1)} copy(bf16[64,4096]{1,0:T(8,128)(2,1)} %project.1) | data formatting | bytes 1048576
where the time goes:
time: 161 us
  Pallas kernels  158 us (98%)
  local copies, waits for them, and re-layouts  3.21 us (2%)
    pallas_call x1, Pallas kernels, local(): pl.pallas_call(functools.partial(attend_kernel, peers, heads), out_shape=...  102 us
    pallas_call x1, Pallas kernels, local(): pl.pallas_call(functools.partial(project_kernel, far), out_shape=jax.Shap...  50.4 us
    pallas_call x1, Pallas kernels, local(): pl.pallas_call(functools.partial(pick_kernel, peers), out_shape=(jax.Shap...  5.74 us

commit v1 on v0

v1 whole, which is shorter than its diff:
```python
import functools

import jax
import jax.numpy as jnp
from jax import lax
from jax.experimental import pallas as pl
from jax.experimental.pallas import tpu as pltpu
from jax.sharding import PartitionSpec as P

MESH = pl.DeviceIdType.MESH
NEG = -1e30
LOG2E = 1.4426950408889634


def pick_kernel(far, ids_ref, slot_ref, len_ref, kv_ref, q_ref, send_ref, lim_ref, idx_ref, qt_ref,
                pick, held_pieces, in_sem, out_sem):
    me = lax.axis_index("req")
    lo = me % 2
    held, _, _, piece_keys, _ = kv_ref.shape
    sel = ids_ref.shape[2]
    pieces = slot_ref.shape[1]
    per = pieces // (2 * far)
    base = me * held
    other = (me + 1 - 2 * lo) * held

    @pl.loop(0, far)
    def _(z):
        for s in range(sel):
            c = ids_ref[z * 2 + 1 - lo, 0, s]
            n = jnp.int32(0)
            for p in range(pieces):
                loc = slot_ref[c, p] - base
                pick[n] = loc
                n = n + ((loc >= 0) & (loc < held)).astype(jnp.int32)
            for j in range(per):
                pltpu.make_async_copy(kv_ref.at[pick[j], 0], held_pieces.at[z, s * per + j], in_sem.at[z]).start()

    groups, _, cols = qt_ref.shape
    tok, heads, _ = q_ref.shape
    per_group = heads // groups
    for h in range(heads):
        at = h % per_group
        qt_ref[h // per_group, :, at * tok:(at + 1) * tok] = q_ref[:, h, :].T

    @pl.loop(0, far)
    def _(z):
        pltpu.make_async_copy(send_ref.at[z], held_pieces.at[z], in_sem.at[z]).wait()
        pltpu.make_async_copy(held_pieces.at[z], send_ref.at[z], out_sem.at[z]).start()

    @pl.loop(0, far)
    def _(z):
        for s in range(sel):
            c = ids_ref[z * 2 + lo, 0, s]
            fill = len_ref[c]
            n = jnp.int32(s * per)
            k = jnp.int32(s * per)
            for p in range(pieces):
                slot = slot_ref[c, p]
                loc = slot - base
                away = slot - other
                left = fill - p * piece_keys
                idx_ref[z, n] = loc
                lim_ref[0, z, n] = left
                n = n + ((loc >= 0) & (loc < held)).astype(jnp.int32)
                lim_ref[1, z, k] = left
                k = k + ((away >= 0) & (away < held)).astype(jnp.int32)

    @pl.loop(0, far)
    def _(z):
        pltpu.make_async_copy(held_pieces.at[z], send_ref.at[z], out_sem.at[z]).wait()


def serve_kernel(far, lim_ref, idx_ref, send_ref, q_ref, k_ref, v_ref, kv_ref, w_ref, out_ref,
                 nbr, qt, kb, vb, top, total, acc, mine, mine_st, came, came_st, full, wv, part, got, low,
                 load_sem, kv_send, kv_recv, q_send, q_recv, p_send, p_recv, s_send, s_recv, a_send, a_recv,
                 wy_send, wy_recv, wx_send, wx_recv, part_send, part_recv, out_send, out_recv):
    me = lax.axis_index("req")
    head = lax.axis_index("head")
    grp = lax.axis_index("groups")
    hi, lo = me // 2, me % 2
    end = far - 1
    pair = {"req": me + 1 - 2 * lo}
    twin = {"groups": grp + 1 - 2 * (grp % 2)}
    mate = {"head": 1 - head}

    tok, hd = k_ref.shape
    count, piece_keys = send_ref.shape[1], send_ref.shape[3]
    keys = count * piece_keys
    groups, _, cols = q_ref.shape
    per_group = cols // tok
    block = min(128, cols)
    factor = hd ** (-0.5) * LOG2E
    half = out_ref.shape[0]
    depth, columns = w_ref.shape
    wide = 2 * columns
    slab = depth // (2 * groups)
    slice_depth = depth // groups

    def at(z):
        return {"req": z * 2 + lo}

    load_q = pltpu.make_async_copy(q_ref, qt.at[hi], load_sem.at[0])
    load_w = pltpu.make_async_copy(w_ref, wv.at[lo], load_sem.at[1])
    load_q.start()
    load_w.start()

    barrier = pltpu.get_barrier_semaphore()
    for k in range(1, far):
        pl.semaphore_signal(barrier, inc=1, device_id=at(lax.rem(hi + k, far)), device_id_type=MESH)
    for device in (pair, twin, mate):
        pl.semaphore_signal(barrier, inc=1, device_id=device, device_id_type=MESH)
    pl.semaphore_wait(barrier, far + 2)

    shorter = jnp.where(hi < end - hi, hi, end - hi)

    def order(i):
        both = i <= 2 * shorter
        d = jnp.where(both, (i + 1) // 2, i - shorter)
        above = jnp.where(both, i % 2 == 1, hi < end - hi)
        return jnp.where(i == far, hi, jnp.where(above, hi + d, hi - d))

    def q_copy(z, g, to, way):
        return pltpu.make_async_remote_copy(
            src_ref=qt.at[z, g], dst_ref=qt.at[z, g], send_sem=q_send.at[way, z, g],
            recv_sem=q_recv.at[z, g], device_id=at(to), device_id_type=MESH)

    def a_copy(z, g, to, way):
        return pltpu.make_async_remote_copy(
            src_ref=full.at[z, g], dst_ref=full.at[z, g], send_sem=a_send.at[way, z, g],
            recv_sem=a_recv.at[z, g], device_id=at(to), device_id_type=MESH)

    def kv_copy(z):
        return pltpu.make_async_remote_copy(
            src_ref=send_ref.at[z], dst_ref=nbr.at[z], send_sem=kv_send.at[z],
            recv_sem=kv_recv.at[z], device_id=pair, device_id_type=MESH)

    def w_rows(which, c):
        return pl.ds(pl.multiple_of((which * groups + c) * slab, slab), slab)

    def wy_copy(c, slot):
        rows = w_rows(grp % 2, c)
        return pltpu.make_async_remote_copy(
            src_ref=w_ref.at[rows], dst_ref=wv.at[slot, rows], send_sem=wy_send.at[c],
            recv_sem=wy_recv.at[c], device_id=pair, device_id_type=MESH)

    def wx_copy(c, which):
        rows = w_rows(which, c)
        return pltpu.make_async_remote_copy(
            src_ref=wv.at[1 - lo, rows], dst_ref=wv.at[1 - lo, rows], send_sem=wx_send.at[c],
            recv_sem=wx_recv.at[c], device_id=twin, device_id_type=MESH)

    def inner(b):
        return jnp.where(hi > b, hi - 1, hi + 1)

    def part_pair(b, g, slot, to):
        return (
            pltpu.make_async_remote_copy(
                src_ref=mine.at[b, g], dst_ref=came.at[slot, g], send_sem=p_send.at[b, g],
                recv_sem=p_recv.at[slot, g], device_id=at(to), device_id_type=MESH),
            pltpu.make_async_remote_copy(
                src_ref=mine_st.at[b, g], dst_ref=came_st.at[slot, g], send_sem=s_send.at[b, g],
                recv_sem=s_recv.at[slot, g], device_id=at(to), device_id_type=MESH))

    def part_start(b, g):
        to = inner(b)
        slot = jnp.where((to == b) & (hi > b), far, b)
        for copy in part_pair(b, g, slot, to):
            copy.start()

    def part_wait(b, g, slot):
        for copy in part_pair(b, g, slot, jnp.where(hi < end, hi + 1, hi - 1)):
            copy.wait_recv()

    load_q.wait()

    @pl.loop(0, groups)
    def _(g):
        @pl.when(hi < end)
        def _():
            q_copy(hi, g, hi + 1, 0).start()

        @pl.when(hi > 0)
        def _():
            q_copy(hi, g, hi - 1, 1).start()

    @pl.loop(1, far + 1)
    def _(i):
        kv_copy(order(i)).start()

    @pl.loop(0, groups)
    def _(c):
        wy_copy(c, lo).start()

    own_vt = v_ref[...].T
    own_k = k_ref[...]

    @pl.loop(0, groups)
    def _(g):
        s = jnp.dot(own_k, qt[hi, g], preferred_element_type=jnp.float32)
        u = lax.broadcasted_iota(jnp.int32, s.shape, 0)
        t = lax.broadcasted_iota(jnp.int32, s.shape, 1) % tok
        s = jnp.where(u <= t, s, NEG)
        m = jnp.max(s, axis=0, keepdims=True)
        w = jnp.exp2((s - m) * factor)
        top[0, g] = m
        total[0, g] = jnp.sum(w, axis=0, keepdims=True)
        acc[0, g] = jnp.dot(own_vt, w.astype(jnp.bfloat16), preferred_element_type=jnp.float32)

    def unit(z, src, slot, g):
        fills = [lim_ref[src, z, i] for i in range(count)]
        key = lax.broadcasted_iota(jnp.int32, (piece_keys, block), 0)

        def score(b):
            s = jnp.dot(kb[src], qt[z, g, :, b * block:(b + 1) * block], preferred_element_type=jnp.float32)
            return jnp.concatenate(
                [jnp.where(key < fills[i], s[i * piece_keys:(i + 1) * piece_keys], NEG) for i in range(count)], axis=0)

        def weigh(b, s):
            at_b = slice(b * block, (b + 1) * block)
            m_old = top[slot, g, :, at_b]
            m = jnp.maximum(m_old, jnp.max(s, axis=0, keepdims=True))
            keep = jnp.exp2((m_old - m) * factor)
            w = jnp.exp2((s - m) * factor)
            mixed = jnp.dot(vb[src], w.astype(jnp.bfloat16), preferred_element_type=jnp.float32)
            top[slot, g, :, at_b] = m
            total[slot, g, :, at_b] = total[slot, g, :, at_b] * keep + jnp.sum(w, axis=0, keepdims=True)
            acc[slot, g, :, at_b] = acc[slot, g, :, at_b] * keep + mixed

        s = score(0)
        for b in range(cols // block):
            ahead = score(b + 1) if b + 1 < cols // block else None
            weigh(b, s)
            s = ahead

    def blend(m1, l1, a1, m2, l2, a2):
        m = jnp.maximum(m1, m2)
        f1 = jnp.exp2((m1 - m) * factor)
        f2 = jnp.exp2((m2 - m) * factor)
        return m, l1 * f1 + l2 * f2, a1 * f1 + a2 * f2

    def merge(b, g):
        part_wait(b, g, b)
        m, l, a = blend(
            mine_st[b, g, 0:1], mine_st[b, g, 1:2], mine[b, g].astype(jnp.float32),
            came_st[b, g, 0:1], came_st[b, g, 1:2], came[b, g].astype(jnp.float32))
        mine_st[b, g, 0:1] = m
        mine_st[b, g, 1:2] = l
        mine[b, g] = a.astype(jnp.bfloat16)
        part_start(b, g)

    def absorb(slot, g):
        part_wait(hi, g, slot)
        m, l, a = blend(
            top[0, g], total[0, g], acc[0, g],
            came_st[slot, g, 0:1], came_st[slot, g, 1:2], came[slot, g].astype(jnp.float32))
        top[0, g] = m
        total[0, g] = l
        acc[0, g] = a

    last = jnp.where(2 * shorter >= 2 * end - far, far, 2 * (end - shorter))

    @pl.loop(0, 2 * end + 1)
    def _(i):
        b = order(i)
        slot = jnp.where(b == hi, 0, 1)

        @pl.when(i < far)
        def _():
            for j in range(count):
                at_j = slice(j * piece_keys, (j + 1) * piece_keys)
                loc = idx_ref[b, j]
                kb[0, at_j] = kv_ref[loc, 0, 0]
                vb[0, :, at_j] = kv_ref[loc, 0, 1].T

            @pl.when(i > 0)
            def _():
                top[1] = jnp.full_like(top[1], NEG)
                total[1] = jnp.zeros_like(total[1])
                acc[1] = jnp.zeros_like(acc[1])

            @pl.loop(0, groups)
            def _(g):
                @pl.when((i > 0) & (hi - i >= 0))
                def _():
                    q_copy(hi - i, g, hi, 0).wait_recv()

                    @pl.when(hi < end)
                    def _():
                        q_copy(hi - i, g, hi + 1, 0).start()

                @pl.when((i > 0) & (hi + i <= end))
                def _():
                    q_copy(hi + i, g, hi, 1).wait_recv()

                    @pl.when(hi > 0)
                    def _():
                        q_copy(hi + i, g, hi - 1, 1).start()

                unit(b, 0, slot, g)

        @pl.when((i > 0) & (i <= far))
        def _():
            kv_copy(b).wait_recv()
            for j in range(count):
                at_j = slice(j * piece_keys, (j + 1) * piece_keys)
                kb[1, at_j] = nbr[b, j, 0]
                vb[1, :, at_j] = nbr[b, j, 1].T

        @pl.loop(0, groups)
        def _(g):
            @pl.when((i > 0) & (i <= far))
            def _():
                unit(b, 1, slot, g)

                @pl.when(i < far)
                def _():
                    mine_st[b, g, 0:1] = top[1, g]
                    mine_st[b, g, 1:2] = total[1, g]
                    mine[b, g] = acc[1, g].astype(jnp.bfloat16)

                    @pl.when(((hi == end) & (b < hi)) | ((hi == 0) & (b > hi)))
                    def _():
                        part_start(b, g)

            low_b = 2 * end - hi - i
            high_b = i - hi

            @pl.when((low_b >= 0) & (low_b < hi) & (hi < end))
            def _():
                merge(low_b, g)

            @pl.when((high_b > hi) & (high_b <= end) & (hi > 0))
            def _():
                merge(high_b, g)

            @pl.when((i == 2 * hi) & (hi > 0))
            def _():
                absorb(hi, g)

            @pl.when((i == 2 * (end - hi)) & (hi < end))
            def _():
                absorb(far, g)

            @pl.when(i == last)
            def _():
                o = acc[0, g] / total[0, g]
                for h in range(per_group):
                    full[hi, g, :, h * hd:(h + 1) * hd] = o[:, h * tok:(h + 1) * tok].T.astype(full.dtype)

                @pl.when(hi < end)
                def _():
                    a_copy(hi, g, hi + 1, 0).start()

                @pl.when(hi > 0)
                def _():
                    a_copy(hi, g, hi - 1, 1).start()

    def part_copy(z):
        return pltpu.make_async_remote_copy(
            src_ref=part.at[z, 1 - head], dst_ref=got.at[z], send_sem=part_send.at[z],
            recv_sem=part_recv.at[z], device_id=mate, device_id_type=MESH)

    def out_copy(z, owner):
        return pltpu.make_async_remote_copy(
            src_ref=low.at[z], dst_ref=out_ref.at[:, pl.ds(pl.multiple_of(owner * wide, wide), wide)],
            send_sem=out_send.at[z], recv_sem=out_recv.at[owner], device_id=at(z), device_id_type=MESH)

    def compute(z, j):
        at_j = pl.ds(pl.multiple_of(j * columns, columns), columns)
        terms = jnp.dot(full[z, 0], wv[j, 0:slice_depth], preferred_element_type=jnp.float32)
        for g in range(1, groups):
            terms += jnp.dot(full[z, g], wv[j, g * slice_depth:(g + 1) * slice_depth],
                             preferred_element_type=jnp.float32)
        part[z, 0, :, at_j] = terms[:half]
        part[z, 1, :, at_j] = terms[half:]

    def finish(z):
        part_copy(z).wait_recv()
        rows = (part[z, head] + got[z]).astype(out_ref.dtype)

        @pl.when(z == hi)
        def _():
            out_ref[:, pl.ds(pl.multiple_of(hi * wide, wide), wide)] = rows

        @pl.when(z != hi)
        def _():
            low[z] = rows
            out_copy(z, hi).start()

    load_w.wait()
    settle = min(2, end)

    @pl.loop(0, far)
    def _(d):
        @pl.when(d > 0)
        def _():
            @pl.loop(0, 2)
            def _(turn):
                above = (turn == 0) == (hi < end - hi)

                @pl.loop(0, groups)
                def _(g):
                    @pl.when(jnp.logical_not(above) & (hi - d >= 0))
                    def _():
                        a_copy(hi - d, g, hi, 0).wait_recv()

                        @pl.when(hi < end)
                        def _():
                            a_copy(hi - d, g, hi + 1, 0).start()

                    @pl.when(above & (hi + d <= end))
                    def _():
                        a_copy(hi + d, g, hi, 1).wait_recv()

                        @pl.when(hi > 0)
                        def _():
                            a_copy(hi + d, g, hi - 1, 1).start()

                    @pl.when((d == 1) & (turn == 0))
                    def _():
                        wy_copy(g, 1 - lo).wait_recv()
                        wx_copy(g, grp % 2).start()

        @pl.when(d == settle)
        def _():
            @pl.loop(0, groups)
            def _(c):
                wx_copy(c, 1 - grp % 2).wait_recv()

            @pl.loop(0, 2 * settle - 1)
            def _(n):
                z = hi - (settle - 1) + n

                @pl.when((z >= 0) & (z < far))
                def _():
                    compute(z, 1 - lo)
                    part_copy(z).start()

        @pl.loop(0, 2)
        def _(side):
            z = hi + d * (2 * side - 1)

            @pl.when((z >= 0) & (z < far) & ((d > 0) | (side == 0)))
            def _():
                compute(z, lo)

                @pl.when(d >= settle)
                def _():
                    compute(z, 1 - lo)
                    part_copy(z).start()

    @pl.loop(0, far)
    def _(d):
        @pl.loop(0, 2)
        def _(side):
            z = hi + d * (2 * side - 1)

            @pl.when((z >= 0) & (z < far) & ((d > 0) | (side == 0)))
            def _():
                finish(z)

    @pl.loop(0, groups)
    def _(g):
        wy_copy(g, lo).wait_send()
        wx_copy(g, grp % 2).wait_send()

    @pl.loop(0, far)
    def _(z):
        kv_copy(z).wait_send()
        part_copy(z).wait_send()

        @pl.loop(0, groups)
        def _(g):
            @pl.when((z <= hi) & (hi < end))
            def _():
                q_copy(z, g, hi + 1, 0).wait_send()
                a_copy(z, g, hi + 1, 0).wait_send()

            @pl.when((z >= hi) & (hi > 0))
            def _():
                q_copy(z, g, hi - 1, 1).wait_send()
                a_copy(z, g, hi - 1, 1).wait_send()

            @pl.when(z != hi)
            def _():
                for copy in part_pair(z, g, z, inner(z)):
                    copy.wait_send()

        @pl.when(z != hi)
        def _():
            out_copy(z, hi).wait_send()
            out_copy(z, z).wait_recv()


def local(queries, new_keys, new_values, cluster_kv, cluster_len, piece_slot, cluster_ids, w_out):
    peers = lax.axis_size("req")
    far = peers // 2
    tok, heads, hd = queries.shape
    held, _, _, piece_keys, _ = cluster_kv.shape
    pieces = piece_slot.shape[1]
    sel = cluster_ids.shape[2]
    count = sel * (pieces // peers)
    groups = min(4, heads)
    cols = heads * tok // groups
    keys = count * piece_keys
    half = tok // lax.axis_size("head")
    depth, columns = w_out.shape
    wide = 2 * columns
    vmem = pl.BlockSpec(memory_space=pltpu.VMEM)
    smem = pl.BlockSpec(memory_space=pltpu.SMEM)
    any_space = pl.BlockSpec(memory_space=pltpu.HBM)
    low_type, dma = jnp.bfloat16, pltpu.SemaphoreType.DMA
    send, lim, idx, qt = pl.pallas_call(
        functools.partial(pick_kernel, far),
        out_shape=(
            jax.ShapeDtypeStruct((far, count, 2, piece_keys, hd), cluster_kv.dtype),
            jax.ShapeDtypeStruct((2, far, count + 1), jnp.int32),
            jax.ShapeDtypeStruct((far, count + 1), jnp.int32),
            jax.ShapeDtypeStruct((groups, hd, cols), queries.dtype),
        ),
        in_specs=[smem, smem, smem, any_space, vmem],
        out_specs=(any_space, smem, smem, vmem),
        scratch_shapes=[
            pltpu.SMEM((pieces + 1,), jnp.int32),
            pltpu.VMEM((far, count, 2, piece_keys, hd), cluster_kv.dtype),
            dma((far,)),
            dma((far,)),
        ],
        name="pick",
    )(cluster_ids, piece_slot, cluster_len, cluster_kv, queries)
    return pl.pallas_call(
        functools.partial(serve_kernel, far),
        out_shape=jax.ShapeDtypeStruct((half, peers * columns), low_type),
        in_specs=[smem, smem, any_space, any_space, vmem, vmem, vmem, any_space],
        out_specs=vmem,
        scratch_shapes=[
            pltpu.VMEM((far, count, 2, piece_keys, hd), cluster_kv.dtype),
            pltpu.VMEM((far, groups, hd, cols), low_type),
            pltpu.VMEM((2, keys, hd), low_type),
            pltpu.VMEM((2, hd, keys), low_type),
            pltpu.VMEM((2, groups, 1, cols), jnp.float32),
            pltpu.VMEM((2, groups, 1, cols), jnp.float32),
            pltpu.VMEM((2, groups, hd, cols), jnp.float32),
            pltpu.VMEM((far, groups, hd, cols), low_type),
            pltpu.VMEM((far, groups, 2, cols), jnp.float32),
            pltpu.VMEM((far + 1, groups, hd, cols), low_type),
            pltpu.VMEM((far + 1, groups, 2, cols), jnp.float32),
            pltpu.VMEM((far, groups, tok, depth // groups), low_type),
            pltpu.VMEM((2, depth, columns), w_out.dtype),
            pltpu.VMEM((far, 2, half, wide), jnp.float32),
            pltpu.VMEM((far, half, wide), jnp.float32),
            pltpu.VMEM((far, half, wide), low_type),
            dma((2,)),
            dma((far,)),
            dma((far,)),
            dma((2, far, groups)),
            dma((far, groups)),
            dma((far, groups)),
            dma((far + 1, groups)),
            dma((far, groups)),
            dma((far + 1, groups)),
            dma((2, far, groups)),
            dma((far, groups)),
            dma((groups,)),
            dma((groups,)),
            dma((groups,)),
            dma((groups,)),
            dma((far,)),
            dma((far,)),
            dma((far,)),
            dma((far,)),
        ],
        compiler_params=pltpu.CompilerParams(
            collective_id=0, has_side_effects=True, vmem_limit_bytes=62 * 2**20),
        name="serve",
    )(lim, idx, send, qt, new_keys[:, 0], new_values[:, 0], cluster_kv, w_out)


def solution(mesh):
    return jax.shard_map(
        local,
        mesh=mesh,
        in_specs=(
            P(("groups", "req"), "head", None),
            P(("groups", "req"), "head", None),
            P(("groups", "req"), "head", None),
            P(("groups", "req"), "head", None, None, None),
            P("groups"),
            P("groups", None),
            P("groups", "head", None),
            P("head", "req"),
        ),
        out_specs=P(("groups", "req", "head"), None),
        check_vma=False,
    )
```

time: 161 us -> 130 us (0.81)
  Pallas kernels: 158 us -> 127 us
    pallas_call x3 -> x2, Pallas kernels: 158 us -> 127 us  [the longest x1 121 us: local(): pl.pallas_call(functools.partial(serve_kernel, far), out_shape=jax.ShapeD...]
where the time goes in v1:
time: 130 us
  Pallas kernels  127 us (98%)
  local copies, waits for them, and re-layouts  3.21 us (2%)
    pallas_call x1, Pallas kernels, local(): pl.pallas_call(functools.partial(serve_kernel, far), out_shape=jax.ShapeD...  121 us
    pallas_call x1, Pallas kernels, local(): pl.pallas_call(functools.partial(pick_kernel, far), out_shape=(jax.ShapeD...  5.81 us
    unnamed x2, local copies, waits for them, and re-layouts  3.21 us

profile of v1, /device:TPU:0, one launch (start us, length us, event | category | flops | bytes accessed | tf_op | source)
XLA Modules:
  0.0 129.7 jit_solution(12310834840542166864)
XLA Ops:
  0.0 1.3 %copy.9.ids_ref = s32[8,1,2]{2,1,0:T(1,128)} copy(s32[8,1,2]{0,2,1:T(2,128)} %param.14) | data formatting | bytes 128 | tf_op args[6]
  1.3 5.8 %pick.1 = (bf16[4,8,2,128,128]{4,3,2,1,0:T(8,128)(2,1)}, s32[2,4,9]{2,1,0:T(4,128)}, s32[4,9]{1,0:T(4,128)}, bf16[4,128,512]{2,1,0:T(8,128)(2,1)}) custom-call(s32[8,1,2]{2,1,0:T(1,128)} %copy.9.ids_ref, s32[16,32]{1,0:T(8,128)} %slot_ref.1, s32[16]{0:T(128)} %len_ref.1, bf16[64,1,2,128,128]{4,3,2,1,0:T(8,128)(2,1)} %kv_ref.3, bf16[128,16,128]{2,1,0:T(8,128)(2,1)} %q_ref.1), custom_call_target="tpu_custom_call" | custom-call | tf_op jit(solution)/shard_map/pick/pallas_call | solution.py:513
  7.2 120.7 %serve.1 = bf16[64,4096]{1,0:T(8,128)(2,1)} custom-call(s32[2,4,9]{2,1,0:T(4,128)} %get-tuple-element.9.lim_ref, s32[4,9]{1,0:T(4,128)} %get-tuple-element.10.idx_ref, bf16[4,8,2,128,128]{4,3,2,1,0:T(8,128)(2,1)} %get-tuple-element.11.send_ref, bf16[4,128,512]{2,1,0:T(8,128)(2,1)} %get-tuple-element.12.q_ref, bf16[128,128]{1,0:T(8,128)(2,1)} %bitcast.2, ...), custom_call_target="tpu_custom_call" | custom-call | tf_op jit(solution)/shard_map/serve/pallas_call | solution.py:531
  127.9 1.9 %copy.11 = bf16[64,4096]{1,0:T(8,128)(2,1)} copy(bf16[64,4096]{1,0:T(8,128)(2,1)} %serve.1) | data formatting | bytes 1048576

commit v2 on v1

--- a/solution.py
+++ b/solution.py
@@ -12,66 +12,8 @@
 LOG2E = 1.4426950408889634
 
 
-def pick_kernel(far, ids_ref, slot_ref, len_ref, kv_ref, q_ref, send_ref, lim_ref, idx_ref, qt_ref,
-                pick, held_pieces, in_sem, out_sem):
-    me = lax.axis_index("req")
-    lo = me % 2
-    held, _, _, piece_keys, _ = kv_ref.shape
-    sel = ids_ref.shape[2]
-    pieces = slot_ref.shape[1]
-    per = pieces // (2 * far)
-    base = me * held
-    other = (me + 1 - 2 * lo) * held
-
-    @pl.loop(0, far)
-    def _(z):
-        for s in range(sel):
-            c = ids_ref[z * 2 + 1 - lo, 0, s]
-            n = jnp.int32(0)
-            for p in range(pieces):
-                loc = slot_ref[c, p] - base
-                pick[n] = loc
-                n = n + ((loc >= 0) & (loc < held)).astype(jnp.int32)
-            for j in range(per):
-                pltpu.make_async_copy(kv_ref.at[pick[j], 0], held_pieces.at[z, s * per + j], in_sem.at[z]).start()
-
-    groups, _, cols = qt_ref.shape
-    tok, heads, _ = q_ref.shape
-    per_group = heads // groups
-    for h in range(heads):
-        at = h % per_group
-        qt_ref[h // per_group, :, at * tok:(at + 1) * tok] = q_ref[:, h, :].T
-
-    @pl.loop(0, far)
-    def _(z):
-        pltpu.make_async_copy(send_ref.at[z], held_pieces.at[z], in_sem.at[z]).wait()
-        pltpu.make_async_copy(held_pieces.at[z], send_ref.at[z], out_sem.at[z]).start()
-
-    @pl.loop(0, far)
-    def _(z):
-        for s in range(sel):
-            c = ids_ref[z * 2 + lo, 0, s]
-            fill = len_ref[c]
-            n = jnp.int32(s * per)
-            k = jnp.int32(s * per)
-            for p in range(pieces):
-                slot = slot_ref[c, p]
-                loc = slot - base
-                away = slot - other
-                left = fill - p * piece_keys
-                idx_ref[z, n] = loc
-                lim_ref[0, z, n] = left
-                n = n + ((loc >= 0) & (loc < held)).astype(jnp.int32)
-                lim_ref[1, z, k] = left
-                k = k + ((away >= 0) & (away < held)).astype(jnp.int32)
-
-    @pl.loop(0, far)
-    def _(z):
-        pltpu.make_async_copy(held_pieces.at[z], send_ref.at[z], out_sem.at[z]).wait()
-
-
-def serve_kernel(far, lim_ref, idx_ref, send_ref, q_ref, k_ref, v_ref, kv_ref, w_ref, out_ref,
-                 nbr, qt, kb, vb, top, total, acc, mine, mine_st, came, came_st, full, wv, part, got, low,
+def serve_kernel(far, ids_ref, slot_ref, len_ref, q_ref, k_ref, v_ref, kv_ref, w_ref, out_ref,
+                 lim_ref, idx_ref, held, gift, nbr, qt, kb, vb, top, total, acc, mine, mine_st, came, came_st, full, wv, part, got, low,
                  load_sem, kv_send, kv_recv, q_send, q_recv, p_send, p_recv, s_send, s_recv, a_send, a_recv,
                  wy_send, wy_recv, wx_send, wx_recv, part_send, part_recv, out_send, out_recv):
     me = lax.axis_index("req")
@@ -84,9 +26,14 @@
     mate = {"head": 1 - head}
 
     tok, hd = k_ref.shape
-    count, piece_keys = send_ref.shape[1], send_ref.shape[3]
+    heads = q_ref.shape[1]
+    count, piece_keys = gift.shape[1], gift.shape[3]
     keys = count * piece_keys
-    groups, _, cols = q_ref.shape
+    _, groups, _, cols = qt.shape
+    sel = ids_ref.shape[0]
+    pieces = slot_ref.shape[1]
+    per = count // sel
+    slots = held.shape[0]
     per_group = cols // tok
     block = min(128, cols)
     factor = hd ** (-0.5) * LOG2E
@@ -99,9 +46,9 @@
     def at(z):
         return {"req": z * 2 + lo}
 
-    load_q = pltpu.make_async_copy(q_ref, qt.at[hi], load_sem.at[0])
+    load_kv = pltpu.make_async_copy(kv_ref, held, load_sem.at[0])
     load_w = pltpu.make_async_copy(w_ref, wv.at[lo], load_sem.at[1])
-    load_q.start()
+    load_kv.start()
     load_w.start()
 
     barrier = pltpu.get_barrier_semaphore()
@@ -109,15 +56,21 @@
         pl.semaphore_signal(barrier, inc=1, device_id=at(lax.rem(hi + k, far)), device_id_type=MESH)
     for device in (pair, twin, mate):
         pl.semaphore_signal(barrier, inc=1, device_id=device, device_id_type=MESH)
-    pl.semaphore_wait(barrier, far + 2)
-
-    shorter = jnp.where(hi < end - hi, hi, end - hi)
+
+    rising = hi < end - hi
+    shorter = jnp.where(rising, hi, end - hi)
+
+    at_end = (hi == 0) | (hi == end)
+
+    ahead = jnp.logical_not(at_end) & (end - 2 * shorter == 1)
 
     def order(i):
-        both = i <= 2 * shorter
-        d = jnp.where(both, (i + 1) // 2, i - shorter)
-        above = jnp.where(both, i % 2 == 1, hi < end - hi)
-        return jnp.where(i == far, hi, jnp.where(above, hi + d, hi - d))
+        i = jnp.where(ahead & ((i == 1) | (i == 2)), 3 - i, i)
+        n = far - i
+        both = n <= 2 * shorter
+        d = jnp.where(both, (n + 1) // 2, n - shorter)
+        above = jnp.where(both, (n % 2 == 1) == rising, rising)
+        return jnp.where((i == 0) | (i == far), hi, jnp.where(above, hi + d, hi - d))
 
     def q_copy(z, g, to, way):
         return pltpu.make_async_remote_copy(
@@ -131,7 +84,7 @@
 
     def kv_copy(z):
         return pltpu.make_async_remote_copy(
-            src_ref=send_ref.at[z], dst_ref=nbr.at[z], send_sem=kv_send.at[z],
+            src_ref=gift.at[z], dst_ref=nbr.at[z], send_sem=kv_send.at[z],
             recv_sem=kv_recv.at[z], device_id=pair, device_id_type=MESH)
 
     def w_rows(which, c):
@@ -171,21 +124,89 @@
         for copy in part_pair(b, g, slot, jnp.where(hi < end, hi + 1, hi - 1)):
             copy.wait_recv()
 
-    load_q.wait()
+    def find(c, base, also=None):
+        locs, lims = [jnp.int32(0)] * per, [jnp.int32(0)] * per
+        n = jnp.int32(0)
+        fill = len_ref[c]
+        for p in range(pieces):
+            loc = slot_ref[c, p] - base
+            hit = (loc >= 0) & (loc < slots)
+            left = fill - p * piece_keys
+            for j in range(per):
+                take = hit & (n == j)
+                locs[j] = jnp.where(take, loc, locs[j])
+                lims[j] = jnp.where(take, left, lims[j])
+            n = n + hit.astype(jnp.int32)
+        return locs, lims
+
+    def plan(z, s):
+        c = ids_ref[s, z * 2 + lo]
+        locs, lims = find(c, me * slots)
+        _, others = find(c, (me + 1 - 2 * lo) * slots)
+        for j in range(per):
+            idx_ref[z, s * per + j] = locs[j]
+            lim_ref[0, z, s * per + j] = lims[j]
+            lim_ref[1, z, s * per + j] = others[j]
+
+    def give(z):
+        found = []
+        for s in range(sel):
+            found += find(ids_ref[s, z * 2 + 1 - lo], me * slots)[0]
+        return found
+
+    def wrap(z, found):
+        for j in range(count):
+            gift[z, j] = held[found[j], 0]
+        kv_copy(z).start()
+
+    for h in range(heads):
+        at_h = h % per_group
+        qt[hi, h // per_group, :, at_h * tok:(at_h + 1) * tok] = q_ref[:, h, :].T
+    found = give(order(1))
+    for s in range(sel):
+        plan(hi, s)
+        plan(order(1), s)
+    pl.semaphore_wait(barrier, far + 2)
+
+    def first(gap):
+        return jnp.where((gap == 0) | (3 * gap >= 2 * groups), groups, (3 * gap + 1) // 2)
+
+    def intake(n, g, upper):
+        above, below = end - n + 1, n - 1
+
+        @pl.when(upper & (above > hi))
+        def _():
+            q_copy(above, g, hi, 1).wait_recv()
+
+            @pl.when(hi > 0)
+            def _():
+                q_copy(above, g, hi - 1, 1).start()
+
+        @pl.when(jnp.logical_not(upper) & (below < hi))
+        def _():
+            q_copy(below, g, hi, 0).wait_recv()
+
+            @pl.when(hi < end)
+            def _():
+                q_copy(below, g, hi + 1, 0).start()
 
     @pl.loop(0, groups)
     def _(g):
-        @pl.when(hi < end)
+        @pl.when((hi < end) & (g < first(hi)))
         def _():
             q_copy(hi, g, hi + 1, 0).start()
 
-        @pl.when(hi > 0)
+        @pl.when((hi > 0) & (g < first(end - hi)))
         def _():
             q_copy(hi, g, hi - 1, 1).start()
 
-    @pl.loop(1, far + 1)
+    load_kv.wait()
+    wrap(order(1), found)
+
+    @pl.loop(2, far + 1)
     def _(i):
-        kv_copy(order(i)).start()
+        z = order(i)
+        wrap(z, give(z))
 
     @pl.loop(0, groups)
     def _(c):
@@ -206,8 +227,8 @@
         total[0, g] = jnp.sum(w, axis=0, keepdims=True)
         acc[0, g] = jnp.dot(own_vt, w.astype(jnp.bfloat16), preferred_element_type=jnp.float32)
 
-    def unit(z, src, slot, g):
-        fills = [lim_ref[src, z, i] for i in range(count)]
+    def unit(z, side, src, slot, g):
+        fills = [lim_ref[side, z, i] for i in range(count)]
         key = lax.broadcasted_iota(jnp.int32, (piece_keys, block), 0)
 
         def score(b):
@@ -257,48 +278,35 @@
         total[0, g] = l
         acc[0, g] = a
 
-    last = jnp.where(2 * shorter >= 2 * end - far, far, 2 * (end - shorter))
-
-    @pl.loop(0, 2 * end + 1)
+    def stage(z, buf):
+        for j in range(count):
+            at_j = slice(j * piece_keys, (j + 1) * piece_keys)
+            loc = idx_ref[z, j]
+            kb[buf, at_j] = held[loc, 0, 0]
+            vb[buf, :, at_j] = held[loc, 0, 1].T
+
+    @pl.loop(0, far + 1)
     def _(i):
         b = order(i)
         slot = jnp.where(b == hi, 0, 1)
+        closing = i == far
+        middle = (i > 0) & (i < far)
 
         @pl.when(i < far)
         def _():
-            for j in range(count):
-                at_j = slice(j * piece_keys, (j + 1) * piece_keys)
-                loc = idx_ref[b, j]
-                kb[0, at_j] = kv_ref[loc, 0, 0]
-                vb[0, :, at_j] = kv_ref[loc, 0, 1].T
-
-            @pl.when(i > 0)
-            def _():
-                top[1] = jnp.full_like(top[1], NEG)
-                total[1] = jnp.zeros_like(total[1])
-                acc[1] = jnp.zeros_like(acc[1])
-
-            @pl.loop(0, groups)
-            def _(g):
-                @pl.when((i > 0) & (hi - i >= 0))
-                def _():
-                    q_copy(hi - i, g, hi, 0).wait_recv()
-
-                    @pl.when(hi < end)
-                    def _():
-                        q_copy(hi - i, g, hi + 1, 0).start()
-
-                @pl.when((i > 0) & (hi + i <= end))
-                def _():
-                    q_copy(hi + i, g, hi, 1).wait_recv()
-
-                    @pl.when(hi > 0)
-                    def _():
-                        q_copy(hi + i, g, hi - 1, 1).start()
-
-                unit(b, 0, slot, g)
-
-        @pl.when((i > 0) & (i <= far))
+            stage(b, 0)
+
+        @pl.when((ahead & (i == 0)) | (jnp.logical_not(ahead) & middle) | (middle & (i > 1)))
+        def _():
+            top[1] = jnp.full_like(top[1], NEG)
+            total[1] = jnp.zeros_like(total[1])
+            acc[1] = jnp.zeros_like(acc[1])
+
+        @pl.when(ahead & (i == 0))
+        def _():
+            stage(order(1), 1)
+
+        @pl.when(i > 0)
         def _():
             kv_copy(b).wait_recv()
             for j in range(count):
@@ -308,22 +316,35 @@
 
         @pl.loop(0, groups)
         def _(g):
-            @pl.when((i > 0) & (i <= far))
-            def _():
-                unit(b, 1, slot, g)
-
-                @pl.when(i < far)
-                def _():
-                    mine_st[b, g, 0:1] = top[1, g]
-                    mine_st[b, g, 1:2] = total[1, g]
-                    mine[b, g] = acc[1, g].astype(jnp.bfloat16)
-
-                    @pl.when(((hi == end) & (b < hi)) | ((hi == 0) & (b > hi)))
-                    def _():
-                        part_start(b, g)
-
-            low_b = 2 * end - hi - i
-            high_b = i - hi
+            @pl.when(at_end & middle)
+            def _():
+                intake(i, g, hi == 0)
+
+            @pl.when((i < far) & jnp.logical_not(ahead & (i == 1)))
+            def _():
+                unit(b, 0, 0, slot, g)
+
+            @pl.when(ahead & (i == 0))
+            def _():
+                intake(1, g, jnp.logical_not(rising))
+                unit(order(1), 0, 1, 1, g)
+
+            @pl.when(i > 0)
+            def _():
+                unit(b, 1, 1, slot, g)
+
+            @pl.when(middle)
+            def _():
+                mine_st[b, g, 0:1] = top[1, g]
+                mine_st[b, g, 1:2] = total[1, g]
+                mine[b, g] = acc[1, g].astype(jnp.bfloat16)
+
+                @pl.when(at_end)
+                def _():
+                    part_start(b, g)
+
+            low_b = i - 1 - end + hi
+            high_b = far + hi - i
 
             @pl.when((low_b >= 0) & (low_b < hi) & (hi < end))
             def _():
@@ -333,16 +354,16 @@
             def _():
                 merge(high_b, g)
 
-            @pl.when((i == 2 * hi) & (hi > 0))
-            def _():
-                absorb(hi, g)
-
-            @pl.when((i == 2 * (end - hi)) & (hi < end))
-            def _():
-                absorb(far, g)
-
-            @pl.when(i == last)
-            def _():
+            @pl.when(closing)
+            def _():
+                @pl.when(hi > 0)
+                def _():
+                    absorb(hi, g)
+
+                @pl.when(hi < end)
+                def _():
+                    absorb(far, g)
+
                 o = acc[0, g] / total[0, g]
                 for h in range(per_group):
                     full[hi, g, :, h * hd:(h + 1) * hd] = o[:, h * tok:(h + 1) * tok].T.astype(full.dtype)
@@ -354,6 +375,39 @@
                 @pl.when(hi > 0)
                 def _():
                     a_copy(hi, g, hi - 1, 1).start()
+
+            @pl.when(jnp.logical_not(at_end) & (i < end))
+            def _():
+                @pl.when(jnp.logical_not(ahead & (i == 0)))
+                def _():
+                    intake(i + 1, g, jnp.logical_not(rising))
+
+                @pl.when(g > 0)
+                def _():
+                    intake(i + 1, g - 1, rising)
+
+        @pl.when(i == 0)
+        def _():
+            @pl.loop(2, far)
+            def _(k):
+                for s in range(sel):
+                    plan(order(k), s)
+
+        @pl.when(jnp.logical_not(at_end))
+        def _():
+            @pl.when(i < end)
+            def _():
+                intake(i + 1, groups - 1, rising)
+
+            @pl.loop(0, groups)
+            def _(g):
+                @pl.when((i == hi - 1) & (g >= first(hi)))
+                def _():
+                    q_copy(hi, g, hi + 1, 0).start()
+
+                @pl.when((i == end - hi - 1) & (g >= first(end - hi)))
+                def _():
+                    q_copy(hi, g, hi - 1, 1).start()
 
     def part_copy(z):
         return pltpu.make_async_remote_copy(
@@ -364,6 +418,9 @@
         return pltpu.make_async_remote_copy(
             src_ref=low.at[z], dst_ref=out_ref.at[:, pl.ds(pl.multiple_of(owner * wide, wide), wide)],
             send_sem=out_send.at[z], recv_sem=out_recv.at[owner], device_id=at(z), device_id_type=MESH)
+
+    keep_copy = pltpu.make_async_copy(
+        low.at[hi], out_ref.at[:, pl.ds(pl.multiple_of(hi * wide, wide), wide)], load_sem.at[2])
 
     def compute(z, j):
         at_j = pl.ds(pl.multiple_of(j * columns, columns), columns)
@@ -378,13 +435,14 @@
         part_copy(z).wait_recv()
         rows = (part[z, head] + got[z]).astype(out_ref.dtype)
 
+        low[z] = rows
+
         @pl.when(z == hi)
         def _():
-            out_ref[:, pl.ds(pl.multiple_of(hi * wide, wide), wide)] = rows
+            keep_copy.start()
 
         @pl.when(z != hi)
         def _():
-            low[z] = rows
             out_copy(z, hi).start()
 
     load_w.wait()
@@ -394,12 +452,12 @@
     def _(d):
         @pl.when(d > 0)
         def _():
-            @pl.loop(0, 2)
-            def _(turn):
-                above = (turn == 0) == (hi < end - hi)
-
-                @pl.loop(0, groups)
-                def _(g):
+            @pl.loop(0, groups)
+            def _(g):
+                @pl.loop(0, 2)
+                def _(turn):
+                    above = (turn == 0) == rising
+
                     @pl.when(jnp.logical_not(above) & (hi - d >= 0))
                     def _():
                         a_copy(hi - d, g, hi, 0).wait_recv()
@@ -416,10 +474,10 @@
                         def _():
                             a_copy(hi + d, g, hi - 1, 1).start()
 
-                    @pl.when((d == 1) & (turn == 0))
-                    def _():
-                        wy_copy(g, 1 - lo).wait_recv()
-                        wx_copy(g, grp % 2).start()
+                @pl.when(d == 1)
+                def _():
+                    wy_copy(g, 1 - lo).wait_recv()
+                    wx_copy(g, grp % 2).start()
 
         @pl.when(d == settle)
         def _():
@@ -491,12 +549,14 @@
             out_copy(z, hi).wait_send()
             out_copy(z, z).wait_recv()
 
+    keep_copy.wait()
+
 
 def local(queries, new_keys, new_values, cluster_kv, cluster_len, piece_slot, cluster_ids, w_out):
     peers = lax.axis_size("req")
     far = peers // 2
     tok, heads, hd = queries.shape
-    held, _, _, piece_keys, _ = cluster_kv.shape
+    piece_keys = cluster_kv.shape[3]
     pieces = piece_slot.shape[1]
     sel = cluster_ids.shape[2]
     count = sel * (pieces // peers)
@@ -510,30 +570,16 @@
     smem = pl.BlockSpec(memory_space=pltpu.SMEM)
     any_space = pl.BlockSpec(memory_space=pltpu.HBM)
     low_type, dma = jnp.bfloat16, pltpu.SemaphoreType.DMA
-    send, lim, idx, qt = pl.pallas_call(
-        functools.partial(pick_kernel, far),
-        out_shape=(
-            jax.ShapeDtypeStruct((far, count, 2, piece_keys, hd), cluster_kv.dtype),
-            jax.ShapeDtypeStruct((2, far, count + 1), jnp.int32),
-            jax.ShapeDtypeStruct((far, count + 1), jnp.int32),
-            jax.ShapeDtypeStruct((groups, hd, cols), queries.dtype),
-        ),
-        in_specs=[smem, smem, smem, any_space, vmem],
-        out_specs=(any_space, smem, smem, vmem),
-        scratch_shapes=[
-            pltpu.SMEM((pieces + 1,), jnp.int32),
-            pltpu.VMEM((far, count, 2, piece_keys, hd), cluster_kv.dtype),
-            dma((far,)),
-            dma((far,)),
-        ],
-        name="pick",
-    )(cluster_ids, piece_slot, cluster_len, cluster_kv, queries)
     return pl.pallas_call(
         functools.partial(serve_kernel, far),
         out_shape=jax.ShapeDtypeStruct((half, peers * columns), low_type),
-        in_specs=[smem, smem, any_space, any_space, vmem, vmem, vmem, any_space],
-        out_specs=vmem,
+        in_specs=[smem, smem, smem, vmem, vmem, vmem, any_space, any_space],
+        out_specs=any_space,
         scratch_shapes=[
+            pltpu.SMEM((2, far, count), jnp.int32),
+            pltpu.SMEM((far, count), jnp.int32),
+            pltpu.VMEM(cluster_kv.shape, cluster_kv.dtype),
+            pltpu.VMEM((far, count, 2, piece_keys, hd), cluster_kv.dtype),
             pltpu.VMEM((far, count, 2, piece_keys, hd), cluster_kv.dtype),
             pltpu.VMEM((far, groups, hd, cols), low_type),
             pltpu.VMEM((2, keys, hd), low_type),
@@ -550,7 +596,7 @@
             pltpu.VMEM((far, 2, half, wide), jnp.float32),
             pltpu.VMEM((far, half, wide), jnp.float32),
             pltpu.VMEM((far, half, wide), low_type),
-            dma((2,)),
+            dma((3,)),
             dma((far,)),
             dma((far,)),
             dma((2, far, groups)),
@@ -573,7 +619,7 @@
         compiler_params=pltpu.CompilerParams(
             collective_id=0, has_side_effects=True, vmem_limit_bytes=62 * 2**20),
         name="serve",
-    )(lim, idx, send, qt, new_keys[:, 0], new_values[:, 0], cluster_kv, w_out)
+    )(cluster_ids[:, 0].T, piece_slot, cluster_len, queries, new_keys[:, 0], new_values[:, 0], cluster_kv, w_out)
 
 
 def solution(mesh):

time: 130 us -> 110 us (0.85)
  Pallas kernels: 127 us -> 107 us
  local copies, waits for them, and re-layouts: 3.21 us -> 1.87 us
    pallas_call x1, Pallas kernels: 121 us -> 107 us  [local(): pl.pallas_call(functools.partial(serve_kernel, far), out_shape=jax.ShapeD...]
    pallas_call x1 -> x0, Pallas kernels: 5.81 us -> none  [local(): pl.pallas_call(functools.partial(pick_kernel, far), out_shape=(jax.ShapeD...]
    unnamed x2 -> x1, local copies, waits for them, and re-layouts: 3.21 us -> 1.87 us
where the time goes in v2:
time: 110 us; the launch traced here: 109 us
  Pallas kernels  107 us (97%)
  local copies, waits for them, and re-layouts  1.87 us (2%)
    pallas_call x1, Pallas kernels, local(): pl.pallas_call(functools.partial(serve_kernel, far), out_shape=jax.ShapeD...  107 us

profile of v2, /device:TPU:0, one launch (start us, length us, event | category | flops | bytes accessed | tf_op | source)
XLA Modules:
  0.0 108.5 jit_solution(1801588368391403814)
XLA Ops:
  0.0 106.6 %serve.1 = bf16[64,4096]{1,0:T(8,128)(2,1)} custom-call(s32[2,8]{1,0:T(2,128)} %bitcast.7, s32[16,32]{1,0:T(8,128)} %slot_ref.1, s32[16]{0:T(128)} %len_ref.1, bf16[128,16,128]{2,1,0:T(8,128)(2,1)} %q_ref.1, bf16[128,128]{1,0:T(8,128)(2,1)} %bitcast.5, bf16[128,128]{1,0:T(8,128)(2,1)} %bitcast.6, bf16[64,1,2,128,128]{4,3,2,1,0:T(8,128)(2,1)} %kv_ref.1, ...), custom_call_target="tpu_custom_call" | custom-call | tf_op jit(solution)/shard_map/serve/pallas_call | solution.py:573
  106.6 1.9 %copy.10 = bf16[64,4096]{1,0:T(8,128)(2,1)} copy(bf16[64,4096]{1,0:T(8,128)(2,1)} %serve.1) | data formatting | bytes 1048576

commit v3 on v2

--- a/solution.py
+++ b/solution.py
@@ -13,7 +13,7 @@
 
 
 def serve_kernel(far, ids_ref, slot_ref, len_ref, q_ref, k_ref, v_ref, kv_ref, w_ref, out_ref,
-                 lim_ref, idx_ref, held, gift, nbr, qt, kb, vb, top, total, acc, mine, mine_st, came, came_st, full, wv, part, got, low,
+                 lim_ref, idx_ref, held, gift, vt, nbr, qt, kb, vb, top, total, acc, mine, mine_st, came, came_st, full, wv, part, got, low,
                  load_sem, kv_send, kv_recv, q_send, q_recv, p_send, p_recv, s_send, s_recv, a_send, a_recv,
                  wy_send, wy_recv, wx_send, wx_recv, part_send, part_recv, out_send, out_recv):
     me = lax.axis_index("req")
@@ -35,7 +35,7 @@
     per = count // sel
     slots = held.shape[0]
     per_group = cols // tok
-    block = min(128, cols)
+    block = min(256, cols)
     factor = hd ** (-0.5) * LOG2E
     half = out_ref.shape[0]
     depth, columns = w_ref.shape
@@ -74,17 +74,17 @@
 
     def q_copy(z, g, to, way):
         return pltpu.make_async_remote_copy(
-            src_ref=qt.at[z, g], dst_ref=qt.at[z, g], send_sem=q_send.at[way, z, g],
+            src_ref=qt.at[z, g], dst_ref=qt.at[z, g], send_sem=q_send.at[way, z],
             recv_sem=q_recv.at[z, g], device_id=at(to), device_id_type=MESH)
 
     def a_copy(z, g, to, way):
         return pltpu.make_async_remote_copy(
-            src_ref=full.at[z, g], dst_ref=full.at[z, g], send_sem=a_send.at[way, z, g],
+            src_ref=full.at[z, g], dst_ref=full.at[z, g], send_sem=a_send.at[way, z],
             recv_sem=a_recv.at[z, g], device_id=at(to), device_id_type=MESH)
 
     def kv_copy(z):
         return pltpu.make_async_remote_copy(
-            src_ref=gift.at[z], dst_ref=nbr.at[z], send_sem=kv_send.at[z],
+            src_ref=gift.at[z], dst_ref=nbr.at[z], send_sem=kv_send,
             recv_sem=kv_recv.at[z], device_id=pair, device_id_type=MESH)
 
     def w_rows(which, c):
@@ -93,14 +93,18 @@
     def wy_copy(c, slot):
         rows = w_rows(grp % 2, c)
         return pltpu.make_async_remote_copy(
-            src_ref=w_ref.at[rows], dst_ref=wv.at[slot, rows], send_sem=wy_send.at[c],
+            src_ref=w_ref.at[rows], dst_ref=wv.at[slot, rows], send_sem=wy_send,
             recv_sem=wy_recv.at[c], device_id=pair, device_id_type=MESH)
 
     def wx_copy(c, which):
         rows = w_rows(which, c)
         return pltpu.make_async_remote_copy(
-            src_ref=wv.at[1 - lo, rows], dst_ref=wv.at[1 - lo, rows], send_sem=wx_send.at[c],
+            src_ref=wv.at[1 - lo, rows], dst_ref=wv.at[1 - lo, rows], send_sem=wx_send,
             recv_sem=wx_recv.at[c], device_id=twin, device_id_type=MESH)
+
+    def pass_w(c):
+        wy_copy(c, 1 - lo).wait_recv()
+        wx_copy(c, grp % 2).start()
 
     def inner(b):
         return jnp.where(hi > b, hi - 1, hi + 1)
@@ -108,10 +112,10 @@
     def part_pair(b, g, slot, to):
         return (
             pltpu.make_async_remote_copy(
-                src_ref=mine.at[b, g], dst_ref=came.at[slot, g], send_sem=p_send.at[b, g],
+                src_ref=mine.at[b, g], dst_ref=came.at[slot, g], send_sem=p_send.at[b],
                 recv_sem=p_recv.at[slot, g], device_id=at(to), device_id_type=MESH),
             pltpu.make_async_remote_copy(
-                src_ref=mine_st.at[b, g], dst_ref=came_st.at[slot, g], send_sem=s_send.at[b, g],
+                src_ref=mine_st.at[b, g], dst_ref=came_st.at[slot, g], send_sem=s_send.at[b],
                 recv_sem=s_recv.at[slot, g], device_id=at(to), device_id_type=MESH))
 
     def part_start(b, g):
@@ -162,6 +166,7 @@
     for h in range(heads):
         at_h = h % per_group
         qt[hi, h // per_group, :, at_h * tok:(at_h + 1) * tok] = q_ref[:, h, :].T
+    vt[...] = v_ref[...].T
     found = give(order(1))
     for s in range(sel):
         plan(hi, s)
@@ -212,12 +217,8 @@
     def _(c):
         wy_copy(c, lo).start()
 
-    own_vt = v_ref[...].T
-    own_k = k_ref[...]
-
-    @pl.loop(0, groups)
-    def _(g):
-        s = jnp.dot(own_k, qt[hi, g], preferred_element_type=jnp.float32)
+    def begin(g):
+        s = jnp.dot(k_ref[...], qt[hi, g], preferred_element_type=jnp.float32)
         u = lax.broadcasted_iota(jnp.int32, s.shape, 0)
         t = lax.broadcasted_iota(jnp.int32, s.shape, 1) % tok
         s = jnp.where(u <= t, s, NEG)
@@ -225,18 +226,19 @@
         w = jnp.exp2((s - m) * factor)
         top[0, g] = m
         total[0, g] = jnp.sum(w, axis=0, keepdims=True)
-        acc[0, g] = jnp.dot(own_vt, w.astype(jnp.bfloat16), preferred_element_type=jnp.float32)
-
-    def unit(z, side, src, slot, g):
-        fills = [lim_ref[side, z, i] for i in range(count)]
+        acc[0, g] = jnp.dot(vt[...], w.astype(jnp.bfloat16), preferred_element_type=jnp.float32)
+
+    def unit(z, parts, slot, g):
         key = lax.broadcasted_iota(jnp.int32, (piece_keys, block), 0)
-
-        def score(b):
+        steps = [(side, src, b) for side, src in parts for b in range(cols // block)]
+
+        def score(side, src, b):
             s = jnp.dot(kb[src], qt[z, g, :, b * block:(b + 1) * block], preferred_element_type=jnp.float32)
             return jnp.concatenate(
-                [jnp.where(key < fills[i], s[i * piece_keys:(i + 1) * piece_keys], NEG) for i in range(count)], axis=0)
-
-        def weigh(b, s):
+                [jnp.where(key < lim_ref[side, z, i], s[i * piece_keys:(i + 1) * piece_keys], NEG)
+                 for i in range(count)], axis=0)
+
+        def weigh(src, b, s):
             at_b = slice(b * block, (b + 1) * block)
             m_old = top[slot, g, :, at_b]
             m = jnp.maximum(m_old, jnp.max(s, axis=0, keepdims=True))
@@ -247,11 +249,11 @@
             total[slot, g, :, at_b] = total[slot, g, :, at_b] * keep + jnp.sum(w, axis=0, keepdims=True)
             acc[slot, g, :, at_b] = acc[slot, g, :, at_b] * keep + mixed
 
-        s = score(0)
-        for b in range(cols // block):
-            ahead = score(b + 1) if b + 1 < cols // block else None
-            weigh(b, s)
-            s = ahead
+        s = score(*steps[0])
+        for n, (_, src, b) in enumerate(steps):
+            later = score(*steps[n + 1]) if n + 1 < len(steps) else None
+            weigh(src, b, s)
+            s = later
 
     def blend(m1, l1, a1, m2, l2, a2):
         m = jnp.maximum(m1, m2)
@@ -320,18 +322,25 @@
             def _():
                 intake(i, g, hi == 0)
 
-            @pl.when((i < far) & jnp.logical_not(ahead & (i == 1)))
-            def _():
-                unit(b, 0, 0, slot, g)
+            alone = (i == far) | (ahead & (i == 1))
+
+            @pl.when(i == 0)
+            def _():
+                begin(g)
+                unit(b, [(0, 0)], slot, g)
 
             @pl.when(ahead & (i == 0))
             def _():
                 intake(1, g, jnp.logical_not(rising))
-                unit(order(1), 0, 1, 1, g)
-
-            @pl.when(i > 0)
-            def _():
-                unit(b, 1, 1, slot, g)
+                unit(order(1), [(0, 1)], 1, g)
+
+            @pl.when(alone)
+            def _():
+                unit(b, [(1, 1)], slot, g)
+
+            @pl.when((i > 0) & jnp.logical_not(alone))
+            def _():
+                unit(b, [(0, 0), (1, 1)], slot, g)
 
             @pl.when(middle)
             def _():
@@ -376,15 +385,23 @@
                 def _():
                     a_copy(hi, g, hi - 1, 1).start()
 
-            @pl.when(jnp.logical_not(at_end) & (i < end))
-            def _():
-                @pl.when(jnp.logical_not(ahead & (i == 0)))
+                @pl.when(g == groups - 1)
+                def _():
+                    pass_w(0)
+
+            @pl.when(jnp.logical_not(at_end))
+            def _():
+                @pl.when((i < end) & jnp.logical_not(ahead & (i == 0)))
                 def _():
                     intake(i + 1, g, jnp.logical_not(rising))
 
-                @pl.when(g > 0)
+                @pl.when((i < end) & (g > 0))
                 def _():
                     intake(i + 1, g - 1, rising)
+
+                @pl.when((i > 0) & (i <= end) & (g == 0))
+                def _():
+                    intake(i, groups - 1, rising)
 
         @pl.when(i == 0)
         def _():
@@ -395,10 +412,6 @@
 
         @pl.when(jnp.logical_not(at_end))
         def _():
-            @pl.when(i < end)
-            def _():
-                intake(i + 1, groups - 1, rising)
-
             @pl.loop(0, groups)
             def _(g):
                 @pl.when((i == hi - 1) & (g >= first(hi)))
@@ -411,13 +424,13 @@
 
     def part_copy(z):
         return pltpu.make_async_remote_copy(
-            src_ref=part.at[z, 1 - head], dst_ref=got.at[z], send_sem=part_send.at[z],
+            src_ref=part.at[z, 1 - head], dst_ref=got.at[z], send_sem=part_send,
             recv_sem=part_recv.at[z], device_id=mate, device_id_type=MESH)
 
     def out_copy(z, owner):
         return pltpu.make_async_remote_copy(
             src_ref=low.at[z], dst_ref=out_ref.at[:, pl.ds(pl.multiple_of(owner * wide, wide), wide)],
-            send_sem=out_send.at[z], recv_sem=out_recv.at[owner], device_id=at(z), device_id_type=MESH)
+            send_sem=out_send, recv_sem=out_recv.at[owner], device_id=at(z), device_id_type=MESH)
 
     keep_copy = pltpu.make_async_copy(
         low.at[hi], out_ref.at[:, pl.ds(pl.multiple_of(hi * wide, wide), wide)], load_sem.at[2])
@@ -474,10 +487,31 @@
                         def _():
                             a_copy(hi + d, g, hi - 1, 1).start()
 
-                @pl.when(d == 1)
-                def _():
-                    wy_copy(g, 1 - lo).wait_recv()
-                    wx_copy(g, grp % 2).start()
+                @pl.when((d == 1) & (g < groups - 1))
+                def _():
+                    pass_w(g + 1)
+
+        def around(reach, act):
+            @pl.loop(0, 2)
+            def _(side):
+                z = hi + reach * (2 * side - 1)
+
+                @pl.when((z >= 0) & (z < far) & ((reach > 0) | (side == 0)))
+                def _():
+                    act(z)
+
+        def within(act):
+            @pl.loop(0, 2 * settle - 1)
+            def _(n):
+                z = hi - (settle - 1) + n
+
+                @pl.when((z >= 0) & (z < far))
+                def _():
+                    act(z)
+
+        def rest(z):
+            compute(z, 1 - lo)
+            part_copy(z).start()
 
         @pl.when(d == settle)
         def _():
@@ -485,68 +519,56 @@
             def _(c):
                 wx_copy(c, 1 - grp % 2).wait_recv()
 
-            @pl.loop(0, 2 * settle - 1)
-            def _(n):
-                z = hi - (settle - 1) + n
-
-                @pl.when((z >= 0) & (z < far))
-                def _():
-                    compute(z, 1 - lo)
-                    part_copy(z).start()
-
-        @pl.loop(0, 2)
-        def _(side):
-            z = hi + d * (2 * side - 1)
-
-            @pl.when((z >= 0) & (z < far) & ((d > 0) | (side == 0)))
-            def _():
-                compute(z, lo)
-
-                @pl.when(d >= settle)
-                def _():
-                    compute(z, 1 - lo)
-                    part_copy(z).start()
-
-    @pl.loop(0, far)
-    def _(d):
-        @pl.loop(0, 2)
-        def _(side):
-            z = hi + d * (2 * side - 1)
-
-            @pl.when((z >= 0) & (z < far) & ((d > 0) | (side == 0)))
-            def _():
-                finish(z)
-
-    @pl.loop(0, groups)
-    def _(g):
-        wy_copy(g, lo).wait_send()
-        wx_copy(g, grp % 2).wait_send()
+            within(rest)
+
+        def whole(z):
+            compute(z, lo)
+
+            @pl.when(d >= settle)
+            def _():
+                rest(z)
+
+        around(d, whole)
+
+        @pl.when(d == settle)
+        def _():
+            within(finish)
+
+        @pl.when(d > settle)
+        def _():
+            around(d - 1, finish)
+
+        @pl.when(d == end)
+        def _():
+            around(d, finish)
+
+    def sent(src, sem):
+        pltpu.make_async_remote_copy(
+            src_ref=src, dst_ref=src, send_sem=sem, recv_sem=load_sem.at[0],
+            device_id=mate, device_id_type=MESH).wait_send()
+
+    sent(w_ref.at[pl.ds(0, groups * slab)], wy_send)
+    sent(w_ref.at[pl.ds(0, groups * slab)], wx_send)
+    sent(gift, kv_send)
+    sent(got, part_send)
+    sent(low.at[pl.ds(0, end)], out_send)
 
     @pl.loop(0, far)
     def _(z):
-        kv_copy(z).wait_send()
-        part_copy(z).wait_send()
-
-        @pl.loop(0, groups)
-        def _(g):
-            @pl.when((z <= hi) & (hi < end))
-            def _():
-                q_copy(z, g, hi + 1, 0).wait_send()
-                a_copy(z, g, hi + 1, 0).wait_send()
-
-            @pl.when((z >= hi) & (hi > 0))
-            def _():
-                q_copy(z, g, hi - 1, 1).wait_send()
-                a_copy(z, g, hi - 1, 1).wait_send()
-
-            @pl.when(z != hi)
-            def _():
-                for copy in part_pair(z, g, z, inner(z)):
-                    copy.wait_send()
+        @pl.when((z <= hi) & (hi < end))
+        def _():
+            sent(qt.at[z], q_send.at[0, z])
+            sent(full.at[z], a_send.at[0, z])
+
+        @pl.when((z >= hi) & (hi > 0))
+        def _():
+            sent(qt.at[z], q_send.at[1, z])
+            sent(full.at[z], a_send.at[1, z])
 
         @pl.when(z != hi)
         def _():
-            out_copy(z, hi).wait_send()
+            sent(mine.at[z], p_send.at[z])
+            sent(mine_st.at[z], s_send.at[z])
             out_copy(z, z).wait_recv()
 
     keep_copy.wait()
@@ -580,6 +602,7 @@
             pltpu.SMEM((far, count), jnp.int32),
             pltpu.VMEM(cluster_kv.shape, cluster_kv.dtype),
             pltpu.VMEM((far, count, 2, piece_keys, hd), cluster_kv.dtype),
+            pltpu.VMEM((hd, tok), low_type),
             pltpu.VMEM((far, count, 2, piece_keys, hd), cluster_kv.dtype),
             pltpu.VMEM((far, groups, hd, cols), low_type),
             pltpu.VMEM((2, keys, hd), low_type),
@@ -597,23 +620,23 @@
             pltpu.VMEM((far, half, wide), jnp.float32),
             pltpu.VMEM((far, half, wide), low_type),
             dma((3,)),
+            dma,
             dma((far,)),
+            dma((2, far)),
+            dma((far, groups)),
             dma((far,)),
-            dma((2, far, groups)),
+            dma((far + 1, groups)),
+            dma((far,)),
+            dma((far + 1, groups)),
+            dma((2, far)),
             dma((far, groups)),
-            dma((far, groups)),
-            dma((far + 1, groups)),
-            dma((far, groups)),
-            dma((far + 1, groups)),
-            dma((2, far, groups)),
-            dma((far, groups)),
+            dma,
             dma((groups,)),
+            dma,
             dma((groups,)),
-            dma((groups,)),
-            dma((groups,)),
+            dma,
             dma((far,)),
-            dma((far,)),
-            dma((far,)),
+            dma,
             dma((far,)),
         ],
         compiler_params=pltpu.CompilerParams(

time: 110 us -> 105 us (0.955); the launches traced: 109 us -> 105 us
  Pallas kernels: 107 us -> 103 us
    pallas_call x1, Pallas kernels: 107 us -> 103 us  [local(): pl.pallas_call(functools.partial(serve_kernel, far), out_shape=jax.ShapeD...]
where the time goes in v3:
time: 105 us
  Pallas kernels  103 us (98%)
  local copies, waits for them, and re-layouts  1.87 us (2%)
    pallas_call x1, Pallas kernels, local(): pl.pallas_call(functools.partial(serve_kernel, far), out_shape=jax.ShapeD...  103 us

profile of v3, /device:TPU:0, one launch (start us, length us, event | category | flops | bytes accessed | tf_op | source)
XLA Modules:
  0.0 105.1 jit_solution(5425708579188822825)
XLA Ops:
  0.0 103.3 %serve.1 = bf16[64,4096]{1,0:T(8,128)(2,1)} custom-call(s32[2,8]{1,0:T(2,128)} %bitcast.7, s32[16,32]{1,0:T(8,128)} %slot_ref.1, s32[16]{0:T(128)} %len_ref.1, bf16[128,16,128]{2,1,0:T(8,128)(2,1)} %q_ref.1, bf16[128,128]{1,0:T(8,128)(2,1)} %bitcast.5, bf16[128,128]{1,0:T(8,128)(2,1)} %bitcast.6, bf16[64,1,2,128,128]{4,3,2,1,0:T(8,128)(2,1)} %kv_ref.1, ...), custom_call_target="tpu_custom_call" | custom-call | tf_op jit(solution)/shard_map/serve/pallas_call | solution.py:595
  103.3 1.9 %copy.10 = bf16[64,4096]{1,0:T(8,128)(2,1)} copy(bf16[64,4096]{1,0:T(8,128)(2,1)} %serve.1) | data formatting | bytes 1048576

commit v4 on v3

--- a/solution.py
+++ b/solution.py
@@ -13,7 +13,7 @@
 
 
 def serve_kernel(far, ids_ref, slot_ref, len_ref, q_ref, k_ref, v_ref, kv_ref, w_ref, out_ref,
-                 lim_ref, idx_ref, held, gift, vt, nbr, qt, kb, vb, top, total, acc, mine, mine_st, came, came_st, full, wv, part, got, low,
+                 lim_ref, idx_ref, held, gift, vt, qv, nbr, qt, kb, vb, top, total, acc, mine, mine_st, came, came_st, full, wv, part, got, low,
                  load_sem, kv_send, kv_recv, q_send, q_recv, p_send, p_recv, s_send, s_recv, a_send, a_recv,
                  wy_send, wy_recv, wx_send, wx_recv, part_send, part_recv, out_send, out_recv):
     me = lax.axis_index("req")
@@ -48,6 +48,8 @@
 
     load_kv = pltpu.make_async_copy(kv_ref, held, load_sem.at[0])
     load_w = pltpu.make_async_copy(w_ref, wv.at[lo], load_sem.at[1])
+    load_q = pltpu.make_async_copy(q_ref, qv, load_sem.at[2])
+    load_q.start()
     load_kv.start()
     load_w.start()
 
@@ -82,10 +84,21 @@
             src_ref=full.at[z, g], dst_ref=full.at[z, g], send_sem=a_send.at[way, z],
             recv_sem=a_recv.at[z, g], device_id=at(to), device_id_type=MESH)
 
-    def kv_copy(z):
+    halves = 1
+    share = count // halves
+
+    def kv_copy(z, n):
+        some = pl.ds(n * share, share)
         return pltpu.make_async_remote_copy(
-            src_ref=gift.at[z], dst_ref=nbr.at[z], send_sem=kv_send,
-            recv_sem=kv_recv.at[z], device_id=pair, device_id_type=MESH)
+            src_ref=gift.at[z, some], dst_ref=nbr.at[z, some], send_sem=kv_send,
+            recv_sem=kv_recv.at[z, n], device_id=pair, device_id_type=MESH)
+
+    def fetch(z, n):
+        kv_copy(z, n).wait_recv()
+        for j in range(n * share, (n + 1) * share):
+            at_j = slice(j * piece_keys, (j + 1) * piece_keys)
+            kb[1, at_j] = nbr[z, j, 0]
+            vb[1, :, at_j] = nbr[z, j, 1].T
 
     def w_rows(which, c):
         return pl.ds(pl.multiple_of((which * groups + c) * slab, slab), slab)
@@ -161,52 +174,55 @@
     def wrap(z, found):
         for j in range(count):
             gift[z, j] = held[found[j], 0]
-        kv_copy(z).start()
-
+        for n in range(halves):
+            kv_copy(z, n).start()
+
+    found = give(order(1))
+    load_q.wait()
     for h in range(heads):
         at_h = h % per_group
-        qt[hi, h // per_group, :, at_h * tok:(at_h + 1) * tok] = q_ref[:, h, :].T
+        qt[hi, h // per_group, :, at_h * tok:(at_h + 1) * tok] = qv[:, h, :].T
+    pl.semaphore_wait(barrier, far + 2)
+
+    def first(gap):
+        return jnp.where((gap == 0) | (2 * gap > groups), groups, 2 * gap)
+
+    def intake(n, g, upper):
+        above, below = end - n + 1, n - 1
+
+        @pl.when(upper & (above > hi))
+        def _():
+            q_copy(above, g, hi, 1).wait_recv()
+
+            @pl.when(hi > 0)
+            def _():
+                q_copy(above, g, hi - 1, 1).start()
+
+        @pl.when(jnp.logical_not(upper) & (below < hi))
+        def _():
+            q_copy(below, g, hi, 0).wait_recv()
+
+            @pl.when(hi < end)
+            def _():
+                q_copy(below, g, hi + 1, 0).start()
+
+    @pl.loop(0, groups)
+    def _(g):
+        @pl.when((hi < end) & (g < first(hi)))
+        def _():
+            q_copy(hi, g, hi + 1, 0).start()
+
+        @pl.when((hi > 0) & (g < first(end - hi)))
+        def _():
+            q_copy(hi, g, hi - 1, 1).start()
+
+    load_kv.wait()
+    wrap(order(1), found)
+
     vt[...] = v_ref[...].T
-    found = give(order(1))
     for s in range(sel):
         plan(hi, s)
         plan(order(1), s)
-    pl.semaphore_wait(barrier, far + 2)
-
-    def first(gap):
-        return jnp.where((gap == 0) | (3 * gap >= 2 * groups), groups, (3 * gap + 1) // 2)
-
-    def intake(n, g, upper):
-        above, below = end - n + 1, n - 1
-
-        @pl.when(upper & (above > hi))
-        def _():
-            q_copy(above, g, hi, 1).wait_recv()
-
-            @pl.when(hi > 0)
-            def _():
-                q_copy(above, g, hi - 1, 1).start()
-
-        @pl.when(jnp.logical_not(upper) & (below < hi))
-        def _():
-            q_copy(below, g, hi, 0).wait_recv()
-
-            @pl.when(hi < end)
-            def _():
-                q_copy(below, g, hi + 1, 0).start()
-
-    @pl.loop(0, groups)
-    def _(g):
-        @pl.when((hi < end) & (g < first(hi)))
-        def _():
-            q_copy(hi, g, hi + 1, 0).start()
-
-        @pl.when((hi > 0) & (g < first(end - hi)))
-        def _():
-            q_copy(hi, g, hi - 1, 1).start()
-
-    load_kv.wait()
-    wrap(order(1), found)
 
     @pl.loop(2, far + 1)
     def _(i):
@@ -230,29 +246,31 @@
 
     def unit(z, parts, slot, g):
         key = lax.broadcasted_iota(jnp.int32, (piece_keys, block), 0)
-        steps = [(side, src, b) for side, src in parts for b in range(cols // block)]
-
-        def score(side, src, b):
-            s = jnp.dot(kb[src], qt[z, g, :, b * block:(b + 1) * block], preferred_element_type=jnp.float32)
+        steps = [(*part, b) for part in parts for b in range(cols // block)]
+
+        def score(side, src, low_j, high_j, b):
+            k = kb[src, low_j * piece_keys:high_j * piece_keys]
+            s = jnp.dot(k, qt[z, g, :, b * block:(b + 1) * block], preferred_element_type=jnp.float32)
             return jnp.concatenate(
-                [jnp.where(key < lim_ref[side, z, i], s[i * piece_keys:(i + 1) * piece_keys], NEG)
-                 for i in range(count)], axis=0)
-
-        def weigh(src, b, s):
+                [jnp.where(key < lim_ref[side, z, low_j + n], s[n * piece_keys:(n + 1) * piece_keys], NEG)
+                 for n in range(high_j - low_j)], axis=0)
+
+        def weigh(src, low_j, high_j, b, s):
             at_b = slice(b * block, (b + 1) * block)
             m_old = top[slot, g, :, at_b]
             m = jnp.maximum(m_old, jnp.max(s, axis=0, keepdims=True))
             keep = jnp.exp2((m_old - m) * factor)
             w = jnp.exp2((s - m) * factor)
-            mixed = jnp.dot(vb[src], w.astype(jnp.bfloat16), preferred_element_type=jnp.float32)
+            v = vb[src, :, low_j * piece_keys:high_j * piece_keys]
+            mixed = jnp.dot(v, w.astype(jnp.bfloat16), preferred_element_type=jnp.float32)
             top[slot, g, :, at_b] = m
             total[slot, g, :, at_b] = total[slot, g, :, at_b] * keep + jnp.sum(w, axis=0, keepdims=True)
             acc[slot, g, :, at_b] = acc[slot, g, :, at_b] * keep + mixed
 
         s = score(*steps[0])
-        for n, (_, src, b) in enumerate(steps):
+        for n, (_, *step) in enumerate(steps):
             later = score(*steps[n + 1]) if n + 1 < len(steps) else None
-            weigh(src, b, s)
+            weigh(*step, s)
             s = later
 
     def blend(m1, l1, a1, m2, l2, a2):
@@ -294,6 +312,18 @@
         closing = i == far
         middle = (i > 0) & (i < far)
 
+        low_b = i - 1 - end + hi
+        high_b = far + hi - i
+
+        def join(g, fresh):
+            @pl.when((low_b >= 0) & (low_b < hi) & (hi < end) & ((low_b == b) == fresh))
+            def _():
+                merge(low_b, g)
+
+            @pl.when((high_b > hi) & (high_b <= end) & (hi > 0) & ((high_b == b) == fresh))
+            def _():
+                merge(high_b, g)
+
         @pl.when(i < far)
         def _():
             stage(b, 0)
@@ -308,13 +338,12 @@
         def _():
             stage(order(1), 1)
 
+        join(0, False)
+
         @pl.when(i > 0)
         def _():
-            kv_copy(b).wait_recv()
-            for j in range(count):
-                at_j = slice(j * piece_keys, (j + 1) * piece_keys)
-                kb[1, at_j] = nbr[b, j, 0]
-                vb[1, :, at_j] = nbr[b, j, 1].T
+            for n in range(halves):
+                fetch(b, n)
 
         @pl.loop(0, groups)
         def _(g):
@@ -322,25 +351,29 @@
             def _():
                 intake(i, g, hi == 0)
 
-            alone = (i == far) | (ahead & (i == 1))
+            alone = closing | (ahead & (i == 1))
+
+            @pl.when(g > 0)
+            def _():
+                join(g, False)
 
             @pl.when(i == 0)
             def _():
                 begin(g)
-                unit(b, [(0, 0)], slot, g)
+                unit(b, [(0, 0, 0, count)], slot, g)
 
             @pl.when(ahead & (i == 0))
             def _():
                 intake(1, g, jnp.logical_not(rising))
-                unit(order(1), [(0, 1)], 1, g)
+                unit(order(1), [(0, 1, 0, count)], 1, g)
 
             @pl.when(alone)
             def _():
-                unit(b, [(1, 1)], slot, g)
-
-            @pl.when((i > 0) & jnp.logical_not(alone))
-            def _():
-                unit(b, [(0, 0), (1, 1)], slot, g)
+                unit(b, [(1, 1, 0, count)], slot, g)
+
+            @pl.when(middle & jnp.logical_not(alone))
+            def _():
+                unit(b, [(0, 0, 0, count), (1, 1, 0, count)], slot, g)
 
             @pl.when(middle)
             def _():
@@ -352,16 +385,7 @@
                 def _():
                     part_start(b, g)
 
-            low_b = i - 1 - end + hi
-            high_b = far + hi - i
-
-            @pl.when((low_b >= 0) & (low_b < hi) & (hi < end))
-            def _():
-                merge(low_b, g)
-
-            @pl.when((high_b > hi) & (high_b <= end) & (hi > 0))
-            def _():
-                merge(high_b, g)
+            join(g, True)
 
             @pl.when(closing)
             def _():
@@ -395,13 +419,17 @@
                 def _():
                     intake(i + 1, g, jnp.logical_not(rising))
 
-                @pl.when((i < end) & (g > 0))
-                def _():
-                    intake(i + 1, g - 1, rising)
-
-                @pl.when((i > 0) & (i <= end) & (g == 0))
-                def _():
-                    intake(i, groups - 1, rising)
+                @pl.when((i == 0) & (g > 0))
+                def _():
+                    intake(1, g - 1, rising)
+
+                @pl.when((i == 1) & (g == 0))
+                def _():
+                    intake(1, groups - 1, rising)
+
+                @pl.when((i > 0) & (i < end))
+                def _():
+                    intake(i + 1, g, rising)
 
         @pl.when(i == 0)
         def _():
@@ -595,7 +623,7 @@
     return pl.pallas_call(
         functools.partial(serve_kernel, far),
         out_shape=jax.ShapeDtypeStruct((half, peers * columns), low_type),
-        in_specs=[smem, smem, smem, vmem, vmem, vmem, any_space, any_space],
+        in_specs=[smem, smem, smem, any_space, vmem, vmem, any_space, any_space],
         out_specs=any_space,
         scratch_shapes=[
             pltpu.SMEM((2, far, count), jnp.int32),
@@ -603,6 +631,7 @@
             pltpu.VMEM(cluster_kv.shape, cluster_kv.dtype),
             pltpu.VMEM((far, count, 2, piece_keys, hd), cluster_kv.dtype),
             pltpu.VMEM((hd, tok), low_type),
+            pltpu.VMEM(queries.shape, low_type),
             pltpu.VMEM((far, count, 2, piece_keys, hd), cluster_kv.dtype),
             pltpu.VMEM((far, groups, hd, cols), low_type),
             pltpu.VMEM((2, keys, hd), low_type),
@@ -621,7 +650,7 @@
             pltpu.VMEM((far, half, wide), low_type),
             dma((3,)),
             dma,
-            dma((far,)),
+            dma((far, 1)),
             dma((2, far)),
             dma((far, groups)),
             dma((far,)),

time: 105 us -> 104 us (level)
    pallas_call x1, Pallas kernels: 103 us -> 102 us  [local(): pl.pallas_call(functools.partial(serve_kernel, far), out_shape=jax.ShapeD...]
where the time goes in v4:
time: 104 us
  Pallas kernels  102 us (98%)
  local copies, waits for them, and re-layouts  1.87 us (2%)
    pallas_call x1, Pallas kernels, local(): pl.pallas_call(functools.partial(serve_kernel, far), out_shape=jax.ShapeD...  102 us

profile of v4, /device:TPU:0, one launch (start us, length us, event | category | flops | bytes accessed | tf_op | source)
XLA Modules:
  0.0 103.8 jit_solution(14806270579912551629)
XLA Ops:
  0.0 101.9 %serve.1 = bf16[64,4096]{1,0:T(8,128)(2,1)} custom-call(s32[2,8]{1,0:T(2,128)} %bitcast.7, s32[16,32]{1,0:T(8,128)} %slot_ref.1, s32[16]{0:T(128)} %len_ref.1, bf16[128,16,128]{2,1,0:T(8,128)(2,1)} %q_ref.1, bf16[128,128]{1,0:T(8,128)(2,1)} %bitcast.5, bf16[128,128]{1,0:T(8,128)(2,1)} %bitcast.6, bf16[64,1,2,128,128]{4,3,2,1,0:T(8,128)(2,1)} %kv_ref.1, ...), custom_call_target="tpu_custom_call" | custom-call | tf_op jit(solution)/shard_map/serve/pallas_call | solution.py:623
  101.9 1.9 %copy.10 = bf16[64,4096]{1,0:T(8,128)(2,1)} copy(bf16[64,4096]{1,0:T(8,128)(2,1)} %serve.1) | data formatting | bytes 1048576

commit v5 on v4

--- a/solution.py
+++ b/solution.py
@@ -669,9 +669,10 @@
             dma((far,)),
         ],
         compiler_params=pltpu.CompilerParams(
-            collective_id=0, has_side_effects=True, vmem_limit_bytes=62 * 2**20),
+            collective_id=0, has_side_effects=True, vmem_limit_bytes=50 * 2**20),
         name="serve",
-    )(cluster_ids[:, 0].T, piece_slot, cluster_len, queries, new_keys[:, 0], new_values[:, 0], cluster_kv, w_out)
+    )(*(pltpu.with_memory_space_constraint(x, pltpu.HBM) for x in (
+        cluster_ids[:, 0].T, piece_slot, cluster_len, queries, new_keys[:, 0], new_values[:, 0], cluster_kv, w_out)))
 
 
 def solution(mesh):

time: 104 us -> 103 us (level)
  local copies, waits for them, and re-layouts: 1.87 us -> 0.8 us
    unnamed x1, local copies, waits for them, and re-layouts: 1.87 us -> 0.8 us
where the time goes in v5:
time: 103 us
  Pallas kernels  102 us (99%)
    pallas_call x1, Pallas kernels, local(): pl.pallas_call(functools.partial(serve_kernel, far), out_shape=jax.ShapeD...  102 us

profile of v5, /device:TPU:0, one launch (start us, length us, event | category | flops | bytes accessed | tf_op | source)
XLA Modules:
  0.0 102.6 jit_solution(7879123681683771285)
XLA Ops:
  0.0 101.8 %serve.1 = bf16[64,4096]{1,0:T(8,128)(2,1)S(1)} custom-call(s32[2,8]{1,0:T(2,128)} %bitcast.7, s32[16,32]{1,0:T(8,128)} %slot_ref.1, s32[16]{0:T(128)} %len_ref.1, bf16[128,16,128]{2,1,0:T(8,128)(2,1)} %q_ref.1, bf16[128,128]{1,0:T(8,128)(2,1)} %bitcast.5, bf16[128,128]{1,0:T(8,128)(2,1)} %bitcast.6, bf16[64,1,2,128,128]{4,3,2,1,0:T(8,128)(2,1)} %kv_ref.1, ...), custom_call_target="tpu_custom_call" | custom-call | tf_op jit(solution)/shard_map/serve/pallas_call | solution.py:623
  101.8 0.8 copy.10

commit v6 on v5

--- a/solution.py
+++ b/solution.py
@@ -13,7 +13,7 @@
 
 
 def serve_kernel(far, ids_ref, slot_ref, len_ref, q_ref, k_ref, v_ref, kv_ref, w_ref, out_ref,
-                 lim_ref, idx_ref, held, gift, vt, qv, nbr, qt, kb, vb, top, total, acc, mine, mine_st, came, came_st, full, wv, part, got, low,
+                 lim_ref, idx_ref, held, gift, vt, qv, new, nbr, qt, kb, vb, top, total, acc, mine, mine_st, came, came_st, full, wv, part, got, low,
                  load_sem, kv_send, kv_recv, q_send, q_recv, p_send, p_recv, s_send, s_recv, a_send, a_recv,
                  wy_send, wy_recv, wx_send, wx_recv, part_send, part_recv, out_send, out_recv):
     me = lax.axis_index("req")
@@ -49,8 +49,12 @@
     load_kv = pltpu.make_async_copy(kv_ref, held, load_sem.at[0])
     load_w = pltpu.make_async_copy(w_ref, wv.at[lo], load_sem.at[1])
     load_q = pltpu.make_async_copy(q_ref, qv, load_sem.at[2])
+    load_k = pltpu.make_async_copy(k_ref, new.at[0], load_sem.at[3])
+    load_v = pltpu.make_async_copy(v_ref, new.at[1], load_sem.at[4])
     load_q.start()
     load_kv.start()
+    load_k.start()
+    load_v.start()
     load_w.start()
 
     barrier = pltpu.get_barrier_semaphore()
@@ -113,7 +117,7 @@
         rows = w_rows(which, c)
         return pltpu.make_async_remote_copy(
             src_ref=wv.at[1 - lo, rows], dst_ref=wv.at[1 - lo, rows], send_sem=wx_send,
-            recv_sem=wx_recv.at[c], device_id=twin, device_id_type=MESH)
+            recv_sem=wx_recv, device_id=twin, device_id_type=MESH)
 
     def pass_w(c):
         wy_copy(c, 1 - lo).wait_recv()
@@ -219,7 +223,9 @@
     load_kv.wait()
     wrap(order(1), found)
 
-    vt[...] = v_ref[...].T
+    load_k.wait()
+    load_v.wait()
+    vt[...] = new[1].T
     for s in range(sel):
         plan(hi, s)
         plan(order(1), s)
@@ -234,7 +240,7 @@
         wy_copy(c, lo).start()
 
     def begin(g):
-        s = jnp.dot(k_ref[...], qt[hi, g], preferred_element_type=jnp.float32)
+        s = jnp.dot(new[0], qt[hi, g], preferred_element_type=jnp.float32)
         u = lax.broadcasted_iota(jnp.int32, s.shape, 0)
         t = lax.broadcasted_iota(jnp.int32, s.shape, 1) % tok
         s = jnp.where(u <= t, s, NEG)
@@ -543,9 +549,10 @@
 
         @pl.when(d == settle)
         def _():
-            @pl.loop(0, groups)
-            def _(c):
-                wx_copy(c, 1 - grp % 2).wait_recv()
+            rows = pl.ds(pl.multiple_of((1 - grp % 2) * groups * slab, slab), groups * slab)
+            pltpu.make_async_remote_copy(
+                src_ref=wv.at[1 - lo, rows], dst_ref=wv.at[1 - lo, rows], send_sem=wx_send,
+                recv_sem=wx_recv, device_id=twin, device_id_type=MESH).wait_recv()
 
             within(rest)
 
@@ -616,14 +623,13 @@
     half = tok // lax.axis_size("head")
     depth, columns = w_out.shape
     wide = 2 * columns
-    vmem = pl.BlockSpec(memory_space=pltpu.VMEM)
     smem = pl.BlockSpec(memory_space=pltpu.SMEM)
     any_space = pl.BlockSpec(memory_space=pltpu.HBM)
     low_type, dma = jnp.bfloat16, pltpu.SemaphoreType.DMA
     return pl.pallas_call(
         functools.partial(serve_kernel, far),
         out_shape=jax.ShapeDtypeStruct((half, peers * columns), low_type),
-        in_specs=[smem, smem, smem, any_space, vmem, vmem, any_space, any_space],
+        in_specs=[smem, smem, smem, any_space, any_space, any_space, any_space, any_space],
         out_specs=any_space,
         scratch_shapes=[
             pltpu.SMEM((2, far, count), jnp.int32),
@@ -632,6 +638,7 @@
             pltpu.VMEM((far, count, 2, piece_keys, hd), cluster_kv.dtype),
             pltpu.VMEM((hd, tok), low_type),
             pltpu.VMEM(queries.shape, low_type),
+            pltpu.VMEM((2, tok, hd), low_type),
             pltpu.VMEM((far, count, 2, piece_keys, hd), cluster_kv.dtype),
             pltpu.VMEM((far, groups, hd, cols), low_type),
             pltpu.VMEM((2, keys, hd), low_type),
@@ -648,7 +655,7 @@
             pltpu.VMEM((far, 2, half, wide), jnp.float32),
             pltpu.VMEM((far, half, wide), jnp.float32),
             pltpu.VMEM((far, half, wide), low_type),
-            dma((3,)),
+            dma((5,)),
             dma,
             dma((far, 1)),
             dma((2, far)),
@@ -662,7 +669,7 @@
             dma,
             dma((groups,)),
             dma,
-            dma((groups,)),
+            dma,
             dma,
             dma((far,)),
             dma,

time: 103 us -> 103 us (level)
  no operation moved by 1% of the time
where the time goes in v6:
time: 103 us
  Pallas kernels  102 us (99%)
    pallas_call x1, Pallas kernels, local(): pl.pallas_call(functools.partial(serve_kernel, far), out_shape=jax.ShapeD...  102 us

profile of v6, /device:TPU:0, one launch (start us, length us, event | category | flops | bytes accessed | tf_op | source)
XLA Modules:
  0.0 102.6 jit_solution(8018379845222795888)
XLA Ops:
  0.0 101.8 %serve.1 = bf16[64,4096]{1,0:T(8,128)(2,1)S(1)} custom-call(s32[2,8]{1,0:T(2,128)} %bitcast.7, s32[16,32]{1,0:T(8,128)} %slot_ref.1, s32[16]{0:T(128)} %len_ref.1, bf16[128,16,128]{2,1,0:T(8,128)(2,1)} %q_ref.1, bf16[128,128]{1,0:T(8,128)(2,1)} %bitcast.5, bf16[128,128]{1,0:T(8,128)(2,1)} %bitcast.6, bf16[64,1,2,128,128]{4,3,2,1,0:T(8,128)(2,1)} %kv_ref.1, ...), custom_call_target="tpu_custom_call" | custom-call | tf_op jit(solution)/shard_map/serve/pallas_call | solution.py:629
  101.8 0.8 copy.10
